TPU v7x, 32 devices: a whole 2x2x4 slice. The times are simulated.
32 devices in a mesh: outer: 8 (over z, x), inner: 4 (over y, core).
Axes of the slice: x: 2, y: 2, z: 4, core: 2. Of those that a mesh axis runs over, the one named last changes fastest.
Arguments:
- fine_input: bfloat16 [6144, 2048], P(('outer', 'inner')), may hold values from -12 to 12
- fine_query: bfloat16 [6144, 1024], P(('outer', 'inner')), may hold values from -4.5 to 4.5
- fine_key: bfloat16 [6144, 1024], P(('outer', 'inner')), may hold values from -4.5 to 4.5
- fine_value: bfloat16 [6144, 1024], P(('outer', 'inner')), may hold values from -6 to 6
- w_fine_out: bfloat16 [1024, 2048], P(None, 'inner'), may hold values from -0.1875 to 0.1875
- norm_gain: float32 [2048], replicated, may hold values from 0.25 to 1.75
- w_query: bfloat16 [2048, 512], P(None, 'inner'), may hold values from -1 to 1
- w_key: bfloat16 [2048, 512], P(None, 'inner'), may hold values from -1 to 1
- w_value: bfloat16 [2048, 512], P(None, 'inner'), may hold values from -0.125 to 0.125
- w_coarse_out: bfloat16 [512, 2048], P('inner'), may hold values from -0.25 to 0.25
Outputs:
- mixed_stream: bfloat16 [6144, 2048], P(('outer', 'inner'))
All inputs are finite; a program needn't handle non-finite values.
Results may differ from a plain program's by a relative error of at most 0.008.
Values may be sent and summed in bfloat16 or wider, within the bound.
No kernel may reach another device: no remote copies, remote signals or barrier semaphores. Data moves between devices by JAX's collectives and lax.ppermute only.
A program may use at most 128 MiB of HBM per device.

v0:
```python
import math

import jax
import jax.numpy as jnp
from jax import lax
from jax.sharding import PartitionSpec as P

HE = 128
WIN = 512
POOL = 8


very_negative = -1e30


def passed_along(block, axis, distance):
    devices = range(lax.axis_size(axis))
    route = [(i - distance, i) for i in devices if i - distance in devices]
    return lax.ppermute(block, axis, route)


def on_device(
    fine_input,
    fine_query,
    fine_key,
    fine_value,
    w_fine_out,
    norm_gain,
    w_query,
    w_key,
    w_value,
    w_coarse_out,
):
    tok_rows, model_width = fine_input.shape
    fine_heads = fine_query.shape[1] // HE
    score_scale = 1.0 / math.sqrt(HE)
    reach_count = (WIN + tok_rows - 1) // tok_rows
    position = lax.axis_index(("outer", "inner"))
    key_list = []
    value_list = []
    for distance in range(reach_count, 0, -1):
        shifted = passed_along((fine_key, fine_value), ("outer", "inner"), distance)
        key_list.append(shifted[0])
        value_list.append(shifted[1])
    key_list.append(fine_key)
    value_list.append(fine_value)
    span = (reach_count + 1) * tok_rows
    key_heads = jnp.concatenate(key_list, axis=0).reshape(span, fine_heads, HE)
    value_heads = jnp.concatenate(value_list, axis=0).reshape(span, fine_heads, HE)
    query_heads = fine_query.reshape(tok_rows, fine_heads, HE)
    scores = (
        jnp.einsum("qhe,khe->hqk", query_heads, key_heads, preferred_element_type=jnp.float32)
        * score_scale
    )
    row_ids = jnp.arange(tok_rows, dtype=jnp.int32)[:, None] + reach_count * tok_rows
    col_ids = jnp.arange(span, dtype=jnp.int32)[None, :]
    gap_rows = row_ids - col_ids
    allowed = (
        (gap_rows >= 0) & (gap_rows < WIN) & ((position - reach_count) * tok_rows + col_ids >= 0)
    )
    masked = jnp.where(allowed[None], scores, very_negative)
    row_max = jnp.max(masked, axis=-1, keepdims=True)
    exp_weights = jnp.where(allowed[None], jnp.exp(scores - row_max), 0.0)
    row_sum = jnp.sum(exp_weights, axis=-1)
    summed = jnp.einsum(
        "hqk,khe->qhe",
        exp_weights.astype(jnp.bfloat16),
        value_heads,
        preferred_element_type=jnp.float32,
    )
    fine_mix = (
        (summed / jnp.transpose(row_sum)[:, :, None])
        .astype(jnp.bfloat16)
        .reshape(tok_rows, fine_heads * HE)
    )
    projected = jnp.dot(
        fine_mix,
        lax.all_gather(w_fine_out, "inner", axis=1, tiled=True),
        preferred_element_type=jnp.float32,
    )
    fine_state = (fine_input.astype(jnp.float32) + projected).astype(jnp.bfloat16)
    edge_rows = passed_along(fine_state[tok_rows - POOL + 1 :], ("outer", "inner"), 1)
    first_pool = (
        jnp.sum(edge_rows, axis=0, dtype=jnp.float32) + fine_state[0].astype(jnp.float32)
    ) / POOL
    later_pools = (
        jnp.sum(
            fine_state[1 : tok_rows - POOL + 1].reshape(tok_rows // POOL - 1, POOL, model_width),
            axis=1,
            dtype=jnp.float32,
        )
        / POOL
    )
    pooled = jnp.concatenate([first_pool[None], later_pools], axis=0).astype(jnp.bfloat16)
    pooled_wide = pooled.astype(jnp.float32)
    moment = jnp.mean(pooled_wide * pooled_wide, axis=-1, keepdims=True)
    normed = (pooled_wide * lax.rsqrt(moment + 1e-06) * norm_gain).astype(jnp.bfloat16)
    local_heads = w_query.shape[1] // HE
    head_width = local_heads * HE
    joined_weights = jnp.concatenate([w_query, w_key, w_value], axis=1)
    projections = jnp.dot(
        lax.all_gather(normed, "inner", axis=0, tiled=True),
        joined_weights,
        preferred_element_type=jnp.float32,
    ).astype(jnp.bfloat16)
    group_len = projections.shape[0]
    coarse_query = projections[:, :head_width].reshape(group_len, local_heads, HE)
    coarse_key = projections[:, head_width : 2 * head_width]
    coarse_value = projections[:, 2 * head_width :]
    outer_index = lax.axis_index("outer")
    query_pos = outer_index * group_len + jnp.arange(group_len, dtype=jnp.int32)
    pieces = (
        lax.all_gather(coarse_key, "outer", axis=0, tiled=True),
        lax.all_gather(coarse_value, "outer", axis=0, tiled=True),
    )
    prior_max = jnp.full((local_heads, group_len), very_negative, jnp.float32)
    count = pieces[0].shape[0]
    block_keys = pieces[0].reshape(count, local_heads, HE)
    block_values = pieces[1].reshape(count, local_heads, HE)
    block_scores = (
        jnp.einsum("qhe,khe->hqk", coarse_query, block_keys, preferred_element_type=jnp.float32)
        * score_scale
    )
    key_pos = jnp.arange(count, dtype=jnp.int32)
    visible = (key_pos[None, :] <= query_pos[:, None])[None]
    block_masked = jnp.where(visible, block_scores, very_negative)
    new_max = jnp.maximum(prior_max, jnp.max(block_masked, axis=-1))
    block_exp = jnp.where(visible, jnp.exp(block_scores - new_max[:, :, None]), 0.0)
    new_sum = jnp.sum(block_exp, axis=-1)
    contrib = jnp.einsum(
        "hqk,khe->hqe",
        block_exp.astype(jnp.bfloat16),
        block_values,
        preferred_element_type=jnp.float32,
    )
    coarse_mix = (
        jnp.transpose(contrib / new_sum[:, :, None], (1, 0, 2))
        .reshape(group_len, head_width)
        .astype(jnp.bfloat16)
    )
    head_total = lax.psum_scatter(
        jnp.dot(coarse_mix, w_coarse_out, preferred_element_type=jnp.float32).astype(jnp.bfloat16),
        "inner",
        scatter_dimension=0,
        tiled=True,
    ).astype(jnp.float32)
    coarse_out = (pooled_wide + head_total).astype(jnp.bfloat16)
    fine_groups = fine_state.reshape(tok_rows // POOL, POOL, model_width).astype(jnp.float32)
    lifted = fine_groups + coarse_out.astype(jnp.float32)[:, None, :]
    return lifted.reshape(tok_rows, model_width).astype(jnp.bfloat16)


def solution(mesh):
    placed = (
        P(("outer", "inner"), None),
        P(("outer", "inner"), None),
        P(("outer", "inner"), None),
        P(("outer", "inner"), None),
        P(None, "inner"),
        P(),
        P(None, "inner"),
        P(None, "inner"),
        P(None, "inner"),
        P("inner", None),
    )
    return jax.shard_map(
        on_device,
        mesh=mesh,
        in_specs=placed,
        out_specs=P(("outer", "inner"), None),
        check_vma=False,
    )
```

profile of v0, /device:TPU:0, one launch (start us, length us, event | category | flops | bytes accessed | tf_op | source)
XLA Modules:
  0.0 202.3 jit_solution(12393071811701069702)
XLA Ops:
  6.5 0.7 all-gather.2.cloned.1.call-update
  7.3 1.2 copy.16
  8.5 4.4 %collective-permute-start.3 = (bf16[192,1024]{0,1:T(8,128)(2,1)S(1)}, bf16[192,1024]{0,1:T(8,128)(2,1)S(1)}, u32[]{:S(2)}, u32[]{:S(2)}) collective-permute-start(bf16[192,1024]{0,1:T(8,128)(2,1)S(1)} %copy.16), channel_id=1, source_target_pairs={{0,3},{1,4},{2,5},{3,6},{4,7},{5,8},{6,9},{7,10},{8,11},{9,12},{10... | collective-permute-start | bytes 1179656 | tf_op jit(solution)/shard_map/ppermute | solution.py:19
  12.9 3.4 %collective-permute-start.4 = (bf16[192,1024]{0,1:T(8,128)(2,1)S(1)}, bf16[192,1024]{0,1:T(8,128)(2,1)S(1)}, u32[]{:S(2)}, u32[]{:S(2)}) collective-permute-start(bf16[192,1024]{0,1:T(8,128)(2,1)S(1)} %copy.16), channel_id=1, source_target_pairs={{0,2},{1,3},{2,4},{3,5},{4,6},{5,7},{6,8},{7,9},{8,10},{9,11},{10,... | collective-permute-start | bytes 1179656 | tf_op jit(solution)/shard_map/ppermute | solution.py:19
  16.3 3.1 %collective-permute-start.5 = (bf16[192,1024]{0,1:T(8,128)(2,1)S(1)}, bf16[192,1024]{0,1:T(8,128)(2,1)}, u32[]{:S(2)}, u32[]{:S(2)}) collective-permute-start(bf16[192,1024]{0,1:T(8,128)(2,1)S(1)} %copy.16), channel_id=1, source_target_pairs={{0,1},{1,2},{2,3},{3,4},{4,5},{5,6},{6,7},{7,8},{8,9},{9,10},{10,1... | collective-permute-start | bytes 1179656 | tf_op jit(solution)/shard_map/ppermute | solution.py:19
  19.4 1.2 copy.12
  20.6 4.2 %collective-permute-start = (bf16[192,1024]{0,1:T(8,128)(2,1)S(1)}, bf16[192,1024]{0,1:T(8,128)(2,1)}, u32[]{:S(2)}, u32[]{:S(2)}) collective-permute-start(bf16[192,1024]{0,1:T(8,128)(2,1)S(1)} %copy.12), channel_id=1, source_target_pairs={{0,3},{1,4},{2,5},{3,6},{4,7},{5,8},{6,9},{7,10},{8,11},{9,12},{10... | collective-permute-start | bytes 1179656 | tf_op jit(solution)/shard_map/ppermute | solution.py:19
  24.8 4.2 %collective-permute-start.1 = (bf16[192,1024]{0,1:T(8,128)(2,1)S(1)}, bf16[192,1024]{0,1:T(8,128)(2,1)}, u32[]{:S(2)}, u32[]{:S(2)}) collective-permute-start(bf16[192,1024]{0,1:T(8,128)(2,1)S(1)} %copy.12), channel_id=1, source_target_pairs={{0,2},{1,3},{2,4},{3,5},{4,6},{5,7},{6,8},{7,9},{8,10},{9,11},{10,... | collective-permute-start | bytes 1179656 | tf_op jit(solution)/shard_map/ppermute | solution.py:19
  29.1 1.3 collective-permute-start.2
  30.4 0.2 fusion.37
  30.6 16.0 %collective-permute-done.4 = bf16[192,1024]{0,1:T(8,128)(2,1)S(1)} collective-permute-done((bf16[192,1024]{0,1:T(8,128)(2,1)S(1)}, bf16[192,1024]{0,1:T(8,128)(2,1)S(1)}, u32[]{:S(2)}, u32[]{:S(2)}) %collective-permute-start.4) | collective-permute-done | bytes 393248 | tf_op jit(solution)/shard_map/ppermute | solution.py:19
  46.7 0.8 copy-done.3
  47.5 2.1 %pad_maximum_fusion.1 = bf16[768,1024]{0,1:T(8,128)(2,1)S(1)} fusion(bf16[192,1024]{0,1:T(8,128)(2,1)S(1)} %copy.16, bf16[192,1024]{0,1:T(8,128)(2,1)} %collective-permute-done.5, bf16[192,1024]{0,1:T(8,128)(2,1)} %copy-done.3, bf16[192,1024]{0,1:T(8,128)(2,1)} %copy-done.2), kind=kLoop, calls=%fused_computation.16 | loop fusion | flops 6291456 | bytes 3145728 | tf_op jit(solution)/shard_map/concatenate | solution.py:48
  49.6 17.4 %collective-permute-done = bf16[192,1024]{0,1:T(8,128)(2,1)} collective-permute-done((bf16[192,1024]{0,1:T(8,128)(2,1)S(1)}, bf16[192,1024]{0,1:T(8,128)(2,1)}, u32[]{:S(2)}, u32[]{:S(2)}) %collective-permute-start) | collective-permute-done | bytes 393248 | tf_op jit(solution)/shard_map/ppermute | solution.py:19
  67.0 11.2 %collective-permute-done.1 = bf16[192,1024]{0,1:T(8,128)(2,1)} collective-permute-done((bf16[192,1024]{0,1:T(8,128)(2,1)S(1)}, bf16[192,1024]{0,1:T(8,128)(2,1)}, u32[]{:S(2)}, u32[]{:S(2)}) %collective-permute-start.1) | collective-permute-done | bytes 393248 | tf_op jit(solution)/shard_map/ppermute | solution.py:19
  78.2 3.1 %pad_maximum_fusion = bf16[768,1024]{0,1:T(8,128)(2,1)} fusion(bf16[192,1024]{0,1:T(8,128)(2,1)S(1)} %copy.12, bf16[192,1024]{0,1:T(8,128)(2,1)S(1)} %collective-permute-done.2, bf16[192,1024]{0,1:T(8,128)(2,1)} %collective-permute-done.1, bf16[192,1024]{0,1:T(8,128)(2,1)} %collective-permute-done), kind=kLoop, calls=%fused_computation.15 | loop fusion | flops 6291456 | bytes 3145728 | tf_op jit(solution)/shard_map/concatenate | solution.py:49
  81.3 3.7 %fusion.79 = (f32[8,192]{1,0:T(8,128)S(1)}, bf16[8,192,768]{2,1,0:T(8,128)(2,1)}) fusion(pred[192,768]{1,0:T(8,128)(4,1)S(1)} %fusion.37, bf16[768,8,128]{0,2,1:T(8,128)(2,1)S(1)} %bitcast.70, bf16[192,1024]{1,0:T(8,128)(2,1)S(1)} %copy-done.8), kind=kOutput, calls=%fused_computation.83 | convolution fusion | flops 612238080 | bytes 4478976 | tf_op jit(solution)/shard_map/sub | solution.py:63
  85.0 3.0 %fusion.27 = bf16[8,24,8,128]{3,2,1,0:T(8,128)(2,1)S(1)} fusion(bf16[768,8,128]{0,2,1:T(8,128)(2,1)} %bitcast.71, bf16[8,192,768]{2,1,0:T(8,128)(2,1)} %get-tuple-element.8, f32[192,8]{0,1:T(8,128)S(1)} %bitcast.73), kind=kOutput, calls=%fused_computation.29 | convolution fusion | flops 302383104 | bytes 4331520 | tf_op jit(solution)/shard_map/hqk,khe->qhe/dot_general | solution.py:65
  88.1 3.3 %fusion.5 = bf16[192,2048]{1,0:T(8,128)(2,1)S(1)} fusion(bf16[1024,2048]{1,0:T(8,128)(2,1)} %all-gather.2.cloned.1.call-done, bf16[192,2048]{1,0:T(8,128)(2,1)S(1)} %copy-done.1, bf16[8,24,8,128]{3,2,1,0:T(8,128)(2,1)S(1)} %fusion.27), kind=kOutput, calls=%fused_computation.8 | convolution fusion | flops 806486016 | bytes 6160384 | tf_op jit(solution)/shard_map/dot_general | solution.py:76
  91.4 0.5 convert_reduce_fusion
  92.0 5.1 %collective-permute-start.6 = (bf16[7,2048]{1,0:T(8,128)(2,1)S(1)}, bf16[7,2048]{1,0:T(8,128)(2,1)S(1)}, u32[]{:S(2)}, u32[]{:S(2)}) collective-permute-start(bf16[7,2048]{1,0:T(8,128)(2,1)S(1)} %slice.24), channel_id=1, source_target_pairs={{0,1},{1,2},{2,3},{3,4},{4,5},{5,6},{6,7},{7,8},{8,9},{9,10},{10,1... | collective-permute-start | bytes 86024 | tf_op jit(solution)/shard_map/ppermute | solution.py:19
  97.1 0.8 collective-permute-done.6
  98.3 9.8 %all_gather.13 = bf16[96,2048]{1,0:T(8,128)(2,1)S(1)} all-gather(bf16[24,2048]{1,0:T(8,128)(2,1)S(1)} %fusion.57), channel_id=1, replica_groups=mesh['outer'=8,'inner'=4] {'inner'}, dimensions={0}, use_global_device_ids=true | all-gather | bytes 491520 | tf_op jit(solution)/shard_map/all_gather | solution.py:102
  108.1 0.4 fusion.30
  108.5 31.0 %all_gather.14 = bf16[768,128]{1,0:T(8,128)(2,1)S(1)} all-gather(bf16[96,128]{1,0:T(8,128)(2,1)S(1)} %get-tuple-element.5), channel_id=1, replica_groups=mesh['outer'=8,'inner'=4] {'outer'}, dimensions={0}, use_global_device_ids=true | all-gather | bytes 221184 | tf_op jit(solution)/shard_map/all_gather | solution.py:113
  139.5 0.3 select_reduce_fusion
  139.9 30.6 %all_gather.15 = bf16[768,128]{1,0:T(8,128)(2,1)S(1)} all-gather(bf16[96,128]{1,0:T(8,128)(2,1)S(1)} %get-tuple-element.6), channel_id=1, replica_groups=mesh['outer'=8,'inner'=4] {'outer'}, dimensions={0}, use_global_device_ids=true | all-gather | bytes 221184 | tf_op jit(solution)/shard_map/all_gather | solution.py:114
  170.5 0.2 fusion.53
  170.7 1.2 convolution_convert_fusion
  172.0 21.5 %reduce-scatter.2.cloned.1.call-done = bf16[24,2048]{1,0:T(8,128)(2,1)} async-done(((bf16[96,2048]{1,0:T(8,128)(2,1)}), bf16[24,2048]{1,0:T(8,128)(2,1)}) %reduce-scatter.2.cloned.1.call-update) | async-done | bytes 98320 | tf_op jit(solution)/shard_map/reduce_scatter | solution.py:141
  193.4 0.9 fusion.67
  194.4 1.1 fusion.17
  (36 shorter events, 0.5 us)
Async XLA Ops:
  6.5 164.2 %copy-start = (bf16[128,2048]{1,0:T(8,128)(2,1)S(1)}, bf16[128,2048]{1,0:T(8,128)(2,1)}, u32[]{:S(2)}) copy-start(bf16[128,2048]{1,0:T(8,128)(2,1)} %param.19) | copy-start | bytes 1572868
  6.5 81.5 %all-gather.2.cloned.1.call-start = ((), (), s32[]{:S(2)}) async-start(), calls=%async_computation.1 | async-start | bytes 5242880 | tf_op jit(solution)/shard_map/all_gather | solution.py:78
  7.3 186.2 %reduce-scatter.2.cloned.1.call-start = ((), (), s32[]{:S(2)}) async-start(), calls=%async_computation.2 | async-start | bytes 491520 | tf_op jit(solution)/shard_map/reduce_scatter | solution.py:141
  8.5 20.6 %collective-permute-start.3 = (bf16[192,1024]{0,1:T(8,128)(2,1)S(1)}, bf16[192,1024]{0,1:T(8,128)(2,1)S(1)}, u32[]{:S(2)}, u32[]{:S(2)}) collective-permute-start(bf16[192,1024]{0,1:T(8,128)(2,1)S(1)} %copy.16), channel_id=1, source_target_pairs={{0,3},{1,4},{2,5},{3,6},{4,7},{5,8},{6,9},{7,10},{8,11},{9,12},{10... | collective-permute-start | bytes 1179656 | tf_op jit(solution)/shard_map/ppermute | solution.py:19
  12.9 33.8 %collective-permute-start.4 = (bf16[192,1024]{0,1:T(8,128)(2,1)S(1)}, bf16[192,1024]{0,1:T(8,128)(2,1)S(1)}, u32[]{:S(2)}, u32[]{:S(2)}) collective-permute-start(bf16[192,1024]{0,1:T(8,128)(2,1)S(1)} %copy.16), channel_id=1, source_target_pairs={{0,2},{1,3},{2,4},{3,5},{4,6},{5,7},{6,8},{7,9},{8,10},{9,11},{10,... | collective-permute-start | bytes 1179656 | tf_op jit(solution)/shard_map/ppermute | solution.py:19
  16.3 31.2 %collective-permute-start.5 = (bf16[192,1024]{0,1:T(8,128)(2,1)S(1)}, bf16[192,1024]{0,1:T(8,128)(2,1)}, u32[]{:S(2)}, u32[]{:S(2)}) collective-permute-start(bf16[192,1024]{0,1:T(8,128)(2,1)S(1)} %copy.16), channel_id=1, source_target_pairs={{0,1},{1,2},{2,3},{3,4},{4,5},{5,6},{6,7},{7,8},{8,9},{9,10},{10,1... | collective-permute-start | bytes 1179656 | tf_op jit(solution)/shard_map/ppermute | solution.py:19
  20.6 46.3 %collective-permute-start = (bf16[192,1024]{0,1:T(8,128)(2,1)S(1)}, bf16[192,1024]{0,1:T(8,128)(2,1)}, u32[]{:S(2)}, u32[]{:S(2)}) collective-permute-start(bf16[192,1024]{0,1:T(8,128)(2,1)S(1)} %copy.12), channel_id=1, source_target_pairs={{0,3},{1,4},{2,5},{3,6},{4,7},{5,8},{6,9},{7,10},{8,11},{9,12},{10... | collective-permute-start | bytes 1179656 | tf_op jit(solution)/shard_map/ppermute | solution.py:19
  24.8 53.4 %collective-permute-start.1 = (bf16[192,1024]{0,1:T(8,128)(2,1)S(1)}, bf16[192,1024]{0,1:T(8,128)(2,1)}, u32[]{:S(2)}, u32[]{:S(2)}) collective-permute-start(bf16[192,1024]{0,1:T(8,128)(2,1)S(1)} %copy.12), channel_id=1, source_target_pairs={{0,2},{1,3},{2,4},{3,5},{4,6},{5,7},{6,8},{7,9},{8,10},{9,11},{10,... | collective-permute-start | bytes 1179656 | tf_op jit(solution)/shard_map/ppermute | solution.py:19
  29.1 17.6 %copy-start.2 = (bf16[192,1024]{0,1:T(8,128)(2,1)}, bf16[192,1024]{0,1:T(8,128)(2,1)S(1)}, u32[]{:S(2)}) copy-start(bf16[192,1024]{0,1:T(8,128)(2,1)S(1)} %collective-permute-done.3) | copy-start | bytes 1179652
  29.1 49.1 %collective-permute-start.2 = (bf16[192,1024]{0,1:T(8,128)(2,1)S(1)}, bf16[192,1024]{0,1:T(8,128)(2,1)S(1)}, u32[]{:S(2)}, u32[]{:S(2)}) collective-permute-start(bf16[192,1024]{0,1:T(8,128)(2,1)S(1)} %copy.12), channel_id=1, source_target_pairs={{0,1},{1,2},{2,3},{3,4},{4,5},{5,6},{6,7},{7,8},{8,9},{9,10},{10,1... | collective-permute-start | bytes 1179656 | tf_op jit(solution)/shard_map/ppermute | solution.py:19
  46.7 0.8 copy-start.3
  49.6 31.8 %copy-start.8 = (bf16[192,1024]{1,0:T(8,128)(2,1)S(1)}, bf16[192,1024]{1,0:T(8,128)(2,1)}, u32[]{:S(2)}) copy-start(bf16[192,1024]{1,0:T(8,128)(2,1)} %param.11) | copy-start | bytes 1179652
  85.0 3.0 %copy-start.1 = (bf16[192,2048]{1,0:T(8,128)(2,1)S(1)}, bf16[192,2048]{1,0:T(8,128)(2,1)}, u32[]{:S(2)}) copy-start(bf16[192,2048]{1,0:T(8,128)(2,1)} %param.10) | copy-start | bytes 2359300
  88.0 10.1 %copy-start.4 = (f32[2048]{0:T(1024)S(1)}, f32[2048]{0:T(1024)}, u32[]{:S(2)}) copy-start(f32[2048]{0:T(1024)} %param.15) | copy-start | bytes 24580
  88.0 20.0 %copy-start.5 = (bf16[2048,128]{1,0:T(8,128)(2,1)S(1)}, bf16[2048,128]{1,0:T(8,128)(2,1)}, u32[]{:S(2)}) copy-start(bf16[2048,128]{1,0:T(8,128)(2,1)} %param.18) | copy-start | bytes 1572868
  88.1 20.0 %copy-start.6 = (bf16[2048,128]{1,0:T(8,128)(2,1)S(1)}, bf16[2048,128]{1,0:T(8,128)(2,1)}, u32[]{:S(2)}) copy-start(bf16[2048,128]{1,0:T(8,128)(2,1)} %param.17) | copy-start | bytes 1572868
  88.1 20.0 %copy-start.7 = (bf16[2048,128]{1,0:T(8,128)(2,1)S(1)}, bf16[2048,128]{1,0:T(8,128)(2,1)}, u32[]{:S(2)}) copy-start(bf16[2048,128]{1,0:T(8,128)(2,1)} %param.16) | copy-start | bytes 1572868
  92.0 6.0 %collective-permute-start.6 = (bf16[7,2048]{1,0:T(8,128)(2,1)S(1)}, bf16[7,2048]{1,0:T(8,128)(2,1)S(1)}, u32[]{:S(2)}, u32[]{:S(2)}) collective-permute-start(bf16[7,2048]{1,0:T(8,128)(2,1)S(1)} %slice.24), channel_id=1, source_target_pairs={{0,1},{1,2},{2,3},{3,4},{4,5},{5,6},{6,7},{7,8},{8,9},{9,10},{10,1... | collective-permute-start | bytes 86024 | tf_op jit(solution)/shard_map/ppermute | solution.py:19
Sparse Core Ops, SparseCore 0:
  8.9 56.0 all-gather.1
  172.1 21.3 reduce-scatter.1
where the time goes:
time: 203 us; the launch traced here: 202 us
  blocking collectives  71.5 us (35%)
  waiting for transfers between devices  67.7 us (33%)
  starting transfers between devices  25.8 us (13%)
  between operations  13.6 us (7%)
  matrix products  11.9 us (6%)
  other arithmetic  8.52 us (4%)
  local copies, waits for them, and re-layouts  3.27 us (2%)
    ppermute x7, waiting for transfers between devices, passed_along(): return lax.ppermute(block, axis, route)  45.5 us
    all_gather x1, blocking collectives, on_device(): lax.all_gather(coarse_key, 'outer', axis=0, tiled=True)  31 us
    all_gather x1, blocking collectives, on_device(): lax.all_gather(coarse_value, 'outer', axis=0, tiled=True)  30.6 us
    ppermute x7, starting transfers between devices, passed_along(): return lax.ppermute(block, axis, route)  25.7 us
    reduce_scatter x1, waiting for transfers between devices, on_device(): lax.psum_scatter(jnp.dot(coarse_mix, w_coarse_out, preferred_element_type...  21.5 us
    all_gather x1, blocking collectives, on_device(): lax.all_gather(normed, 'inner', axis=0, tiled=True)  9.81 us
  transfers between devices with their start and end apart: 9, of which 5 were waited for; matrix products, arithmetic and copies ran while one was open for 7% of the time, Pallas kernels for 0%

commit v1 on v0

--- a/solution.py
+++ b/solution.py
@@ -17,6 +17,47 @@
     devices = range(lax.axis_size(axis))
     route = [(i - distance, i) for i in devices if i - distance in devices]
     return lax.ppermute(block, axis, route)
+
+
+def swapped_cores(block):
+    count = lax.axis_size("inner")
+    return lax.ppermute(block, "inner", [(i, i ^ 1) for i in range(count)])
+
+
+def columns_of_all(shard):
+    count = lax.axis_size("inner")
+    me = lax.axis_index("inner")
+    rows, width = shard.shape
+    joined = jnp.zeros((rows, count * width), shard.dtype)
+    for hop in range(0, count, 2):
+        near = shard
+        if hop:
+            near = lax.ppermute(shard, "inner", [(i, (i + hop) % count) for i in range(count)])
+        owner = (me - hop) % count
+        joined = lax.dynamic_update_slice(joined, near, (0, owner * width))
+        joined = lax.dynamic_update_slice(joined, swapped_cores(near), (0, (owner ^ 1) * width))
+    return joined
+
+
+def outer_gather(block):
+    count = lax.axis_size("outer")
+    pairs = [[i, i + 1] for i in range(0, count, 2)]
+    lines = [list(range(i, count, 2)) for i in range(2)]
+    near = lax.all_gather(block, "outer", axis=0, tiled=True, axis_index_groups=pairs)
+    return lax.all_gather(near, "outer", axis=0, tiled=True, axis_index_groups=lines)
+
+
+def summed_pieces(block):
+    count = lax.axis_size("inner")
+    me = lax.axis_index("inner")
+    parts = block.reshape(count, block.shape[0] // count, block.shape[1])
+    own = lax.dynamic_index_in_dim(parts, me, 0, keepdims=False).astype(jnp.float32)
+    for hop in range(1, count):
+        piece = lax.dynamic_index_in_dim(parts, me ^ hop, 0, keepdims=False)
+        own = own + lax.ppermute(piece, "inner", [(i, i ^ hop) for i in range(count)]).astype(
+            jnp.float32
+        )
+    return own
 
 
 def on_device(
@@ -36,27 +77,28 @@
     score_scale = 1.0 / math.sqrt(HE)
     reach_count = (WIN + tok_rows - 1) // tok_rows
     position = lax.axis_index(("outer", "inner"))
-    key_list = []
-    value_list = []
+    fine_width = fine_key.shape[1]
+    joined_kv = jnp.concatenate([fine_key, fine_value], axis=1)
+    far_rows = -(-(WIN - (reach_count - 1) * tok_rows) // 16) * 16
+    pieces_kv = []
     for distance in range(reach_count, 0, -1):
-        shifted = passed_along((fine_key, fine_value), ("outer", "inner"), distance)
-        key_list.append(shifted[0])
-        value_list.append(shifted[1])
-    key_list.append(fine_key)
-    value_list.append(fine_value)
-    span = (reach_count + 1) * tok_rows
-    key_heads = jnp.concatenate(key_list, axis=0).reshape(span, fine_heads, HE)
-    value_heads = jnp.concatenate(value_list, axis=0).reshape(span, fine_heads, HE)
+        first = tok_rows - far_rows if distance == reach_count else 0
+        pieces_kv.append(passed_along(joined_kv[first:], ("outer", "inner"), distance))
+    pieces_kv.append(joined_kv)
+    span = reach_count * tok_rows + far_rows
+    all_kv = jnp.concatenate(pieces_kv, axis=0)
+    key_heads = all_kv[:, :fine_width].reshape(span, fine_heads, HE)
+    value_heads = all_kv[:, fine_width:].reshape(span, fine_heads, HE)
     query_heads = fine_query.reshape(tok_rows, fine_heads, HE)
     scores = (
         jnp.einsum("qhe,khe->hqk", query_heads, key_heads, preferred_element_type=jnp.float32)
         * score_scale
     )
-    row_ids = jnp.arange(tok_rows, dtype=jnp.int32)[:, None] + reach_count * tok_rows
+    row_ids = jnp.arange(tok_rows, dtype=jnp.int32)[:, None] + span - tok_rows
     col_ids = jnp.arange(span, dtype=jnp.int32)[None, :]
     gap_rows = row_ids - col_ids
     allowed = (
-        (gap_rows >= 0) & (gap_rows < WIN) & ((position - reach_count) * tok_rows + col_ids >= 0)
+        (gap_rows >= 0) & (gap_rows < WIN) & (position * tok_rows - (span - tok_rows) + col_ids >= 0)
     )
     masked = jnp.where(allowed[None], scores, very_negative)
     row_max = jnp.max(masked, axis=-1, keepdims=True)
@@ -75,7 +117,7 @@
     )
     projected = jnp.dot(
         fine_mix,
-        lax.all_gather(w_fine_out, "inner", axis=1, tiled=True),
+        columns_of_all(w_fine_out),
         preferred_element_type=jnp.float32,
     )
     fine_state = (fine_input.astype(jnp.float32) + projected).astype(jnp.bfloat16)
@@ -105,14 +147,10 @@
     ).astype(jnp.bfloat16)
     group_len = projections.shape[0]
     coarse_query = projections[:, :head_width].reshape(group_len, local_heads, HE)
-    coarse_key = projections[:, head_width : 2 * head_width]
-    coarse_value = projections[:, 2 * head_width :]
     outer_index = lax.axis_index("outer")
     query_pos = outer_index * group_len + jnp.arange(group_len, dtype=jnp.int32)
-    pieces = (
-        lax.all_gather(coarse_key, "outer", axis=0, tiled=True),
-        lax.all_gather(coarse_value, "outer", axis=0, tiled=True),
-    )
+    gathered = outer_gather(projections[:, head_width:])
+    pieces = (gathered[:, :head_width], gathered[:, head_width:])
     prior_max = jnp.full((local_heads, group_len), very_negative, jnp.float32)
     count = pieces[0].shape[0]
     block_keys = pieces[0].reshape(count, local_heads, HE)
@@ -138,12 +176,9 @@
         .reshape(group_len, head_width)
         .astype(jnp.bfloat16)
     )
-    head_total = lax.psum_scatter(
-        jnp.dot(coarse_mix, w_coarse_out, preferred_element_type=jnp.float32).astype(jnp.bfloat16),
-        "inner",
-        scatter_dimension=0,
-        tiled=True,
-    ).astype(jnp.float32)
+    head_total = summed_pieces(
+        jnp.dot(coarse_mix, w_coarse_out, preferred_element_type=jnp.float32).astype(jnp.bfloat16)
+    )
     coarse_out = (pooled_wide + head_total).astype(jnp.bfloat16)
     fine_groups = fine_state.reshape(tok_rows // POOL, POOL, model_width).astype(jnp.float32)
     lifted = fine_groups + coarse_out.astype(jnp.float32)[:, None, :]

time: 203 us -> 119 us (0.59)
  blocking collectives: 71.5 us -> 29.3 us
  waiting for transfers between devices: 67.7 us -> 46.7 us
  between operations: 13.6 us -> 0.31 us
  local copies, waits for them, and re-layouts: 3.27 us -> 12.3 us
  starting transfers between devices: 25.8 us -> 17.8 us
  matrix products: 11.9 us -> 6.15 us
    all_gather x2, blocking collectives: 61.7 us -> 20.1 us  [the longest x1 15.3 us: outer_gather(): lax.all_gather(near, 'outer', axis=0, tiled=True, axis_index_groups=lines)]
    reduce_scatter x1 -> x0, waiting for transfers between devices: 21.5 us -> none  [on_device(): lax.psum_scatter(jnp.dot(coarse_mix, w_coarse_out, preferred_element_type...]
    ppermute x7 -> x4, starting transfers between devices: 25.7 us -> 13.8 us  [passed_along(): return lax.ppermute(block, axis, route)]
    dynamic_update_slice x0 -> x4, local copies, waits for them, and re-layouts: none -> 5.72 us  [the longest x2 3.5 us: columns_of_all(): lax.dynamic_update_slice(joined, swapped_cores(near), (0, (owner ^ 1) * w...]
    ppermute x0 -> x6, waiting for transfers between devices: none -> 5.15 us  [the longest x3 5.14 us: summed_pieces(): lax.ppermute(piece, 'inner', [(i, i ^ hop) for i in range(count)])]
    ppermute x0 -> x6, starting transfers between devices: none -> 3.93 us  [the longest x3 2.2 us: summed_pieces(): lax.ppermute(piece, 'inner', [(i, i ^ hop) for i in range(count)])]
    ppermute x7 -> x4, waiting for transfers between devices: 45.5 us -> 41.6 us  [passed_along(): return lax.ppermute(block, axis, route)]
    sub x1 -> x0, matrix products: 3.7 us -> none  [on_device(): exp_weights = jnp.where(allowed[None], jnp.exp(scores - row_max), 0.0)]
  transfers between devices with their start and end apart: 9 -> 10, of which waited for: 5 -> 4; matrix products, arithmetic and copies ran while one was open for 7% -> 12% of each run, Pallas kernels for 0% -> 0%
where the time goes in v1:
time: 119 us
  waiting for transfers between devices  46.7 us (39%)
  blocking collectives  29.3 us (25%)
  starting transfers between devices  17.8 us (15%)
  local copies, waits for them, and re-layouts  12.3 us (10%)
  other arithmetic  6.57 us (6%)
  matrix products  6.15 us (5%)
    ppermute x4, waiting for transfers between devices, passed_along(): return lax.ppermute(block, axis, route)  41.6 us
    all_gather x1, blocking collectives, outer_gather(): lax.all_gather(near, 'outer', axis=0, tiled=True, axis_index_groups=lines)  15.3 us
    ppermute x4, starting transfers between devices, passed_along(): return lax.ppermute(block, axis, route)  13.8 us
    all_gather x1, blocking collectives, on_device(): lax.all_gather(normed, 'inner', axis=0, tiled=True)  9.25 us
    ppermute x3, waiting for transfers between devices, summed_pieces(): lax.ppermute(piece, 'inner', [(i, i ^ hop) for i in range(count)])  5.14 us
    all_gather x1, blocking collectives, outer_gather(): lax.all_gather(block, 'outer', axis=0, tiled=True, axis_index_groups=pairs)  4.76 us
    dynamic_update_slice x2, local copies, waits for them, and re-layouts, columns_of_all(): lax.dynamic_update_slice(joined, swapped_cores(near), (0, (owner ^ 1) * w...  3.5 us
    dot_general x1, matrix products, on_device(): jnp.dot(fine_mix, columns_of_all(w_fine_out), preferred_element_type=jnp....  3.36 us
  transfers between devices with their start and end apart: 10, of which 4 were waited for; matrix products, arithmetic and copies ran while one was open for 12% of the time, Pallas kernels for 0%

profile of v1, /device:TPU:0, one launch (start us, length us, event | category | flops | bytes accessed | tf_op | source)
XLA Modules:
  0.0 119.1 jit_solution(14035567695519729284)
XLA Ops:
  0.0 1.1 constant_dynamic-update-slice_fusion.1
  1.1 1.1 constant_dynamic-update-slice_fusion
  2.2 3.3 %collective-permute-start.2 = (bf16[192,2048]{1,0:T(8,128)(2,1)S(1)}, bf16[192,2048]{1,0:T(8,128)(2,1)}, u32[]{:S(2)}, u32[]{:S(2)}) collective-permute-start(bf16[192,2048]{1,0:T(8,128)(2,1)S(1)} %constant_dynamic-update-slice_fusion), channel_id=1, source_target_pairs={{0,1},{1,2},{2,3},{3,4},{4,5},{5,6},{6,7},{7,8},{8,9},{9,10},{10,1... | collective-permute-start | bytes 2359304 | tf_op jit(solution)/shard_map/ppermute | solution.py:19
  5.5 4.4 %collective-permute-start.1 = (bf16[192,2048]{1,0:T(8,128)(2,1)S(1)}, bf16[192,2048]{1,0:T(8,128)(2,1)}, u32[]{:S(2)}, u32[]{:S(2)}) collective-permute-start(bf16[192,2048]{1,0:T(8,128)(2,1)S(1)} %constant_dynamic-update-slice_fusion), channel_id=1, source_target_pairs={{0,2},{1,3},{2,4},{3,5},{4,6},{5,7},{6,8},{7,9},{8,10},{9,11},{10,... | collective-permute-start | bytes 2359304 | tf_op jit(solution)/shard_map/ppermute | solution.py:19
  10.0 0.6 collective-permute-start.4
  10.6 1.1 collective-permute-start.3
  11.6 0.8 slice.40
  12.5 3.7 %collective-permute-start = (bf16[128,2048]{1,0:T(8,128)(2,1)}, bf16[128,2048]{1,0:T(8,128)(2,1)}, u32[]{:S(2)}, u32[]{:S(2)}) collective-permute-start(bf16[128,2048]{1,0:T(8,128)(2,1)} %slice.40), channel_id=1, source_target_pairs={{0,3},{1,4},{2,5},{3,6},{4,7},{5,8},{6,9},{7,10},{8,11},{9,12},{10... | collective-permute-start | bytes 1572872 | tf_op jit(solution)/shard_map/ppermute | solution.py:19
  16.1 2.5 %broadcast_in_dim.49 = bf16[1024,2048]{1,0:T(8,128)(2,1)} broadcast(bf16[]{:T(256)} %constant.73.clone.1), dimensions={} | broadcast | bytes 4194306 | tf_op jit(solution)/shard_map/broadcast_in_dim | solution.py:31
  18.6 1.1 constant_dynamic-update-slice_fusion.5
  20.0 40.8 %collective-permute-done = bf16[128,2048]{1,0:T(8,128)(2,1)} collective-permute-done((bf16[128,2048]{1,0:T(8,128)(2,1)}, bf16[128,2048]{1,0:T(8,128)(2,1)}, u32[]{:S(2)}, u32[]{:S(2)}) %collective-permute-start) | collective-permute-done | bytes 524320 | tf_op jit(solution)/shard_map/ppermute | solution.py:19
  60.8 1.7 %pad_maximum_fusion = bf16[704,2048]{1,0:T(8,128)(2,1)S(1)} fusion(bf16[192,2048]{1,0:T(8,128)(2,1)S(1)} %constant_dynamic-update-slice_fusion, bf16[192,2048]{1,0:T(8,128)(2,1)} %collective-permute-done.2, bf16[192,2048]{1,0:T(8,128)(2,1)} %collective-permute-done.1, bf16[128,2048]{1,0:T(8,128)(2,1)} %collective-permute-done), kind=kLoop, calls=%fused_computation.7 | loop fusion | flops 11534336 | bytes 5767168 | tf_op jit(solution)/shard_map/concatenate | solution.py:89
  62.5 0.6 slice_bitcast_fusion.1
  63.5 0.8 fusion.20
  64.3 2.4 %fusion.85 = (f32[8,192]{1,0:T(8,128)S(1)}, bf16[8,192,704]{2,1,0:T(8,128)(2,1)S(1)}) fusion(f32[8,704,192]{1,2,0:T(8,128)S(1)} %fusion.20, pred[192,704]{1,0:T(8,128)(4,1)S(1)} %fusion.50), kind=kOutput, calls=%fused_computation.98 | output fusion | flops 7570111 | bytes 6629376 | tf_op jit(solution)/shard_map/sub | solution.py:105
  66.8 0.8 fusion.38
  67.6 2.4 %constant_dynamic-update-slice_fusion.4 = bf16[1024,2048]{1,0:T(8,128)(2,1)} fusion(bf16[1024,2048]{1,0:T(8,128)(2,1)} %constant_dynamic-update-slice_fusion.5, bf16[1024,512]{1,0:T(8,128)(2,1)} %collective-permute-done.3, s32[]{:T(128)S(6)} %select_n.56), kind=kLoop, calls=%fused_computation.88 | loop fusion | bytes 2097156 | tf_op jit(solution)/shard_map/dynamic_update_slice | solution.py:38
  70.0 1.1 constant_dynamic-update-slice_fusion.3
  71.1 1.1 constant_dynamic-update-slice_fusion.2
  72.2 3.4 %fusion.5 = bf16[192,2048]{1,0:T(8,128)(2,1)S(1)} fusion(bf16[1024,2048]{1,0:T(8,128)(2,1)} %constant_dynamic-update-slice_fusion.2, bf16[192,2048]{1,0:T(8,128)(2,1)S(1)} %copy-done.2, bf16[8,24,8,128]{3,2,1,0:T(8,128)(2,1)S(1)} %fusion.38), kind=kOutput, calls=%fused_computation.9 | convolution fusion | flops 806486016 | bytes 6160384 | tf_op jit(solution)/shard_map/dot_general | solution.py:118
  75.6 0.5 convert_reduce_fusion
  76.2 2.4 %collective-permute-start.6 = (bf16[7,2048]{1,0:T(8,128)(2,1)S(1)}, bf16[7,2048]{1,0:T(8,128)(2,1)S(1)}, u32[]{:S(2)}, u32[]{:S(2)}) collective-permute-start(bf16[7,2048]{1,0:T(8,128)(2,1)S(1)} %slice.43), channel_id=1, source_target_pairs={{0,1},{1,2},{2,3},{3,4},{4,5},{5,6},{6,7},{7,8},{8,9},{9,10},{10,1... | collective-permute-start | bytes 86024 | tf_op jit(solution)/shard_map/ppermute | solution.py:19
  78.6 0.8 collective-permute-done.6
  79.7 9.2 %all_gather.9 = bf16[96,2048]{1,0:T(8,128)(2,1)S(1)} all-gather(bf16[24,2048]{1,0:T(8,128)(2,1)S(1)} %fusion.59), channel_id=1, replica_groups=mesh['outer'=8,'inner'=4] {'inner'}, dimensions={0}, use_global_device_ids=true | all-gather | bytes 491520 | tf_op jit(solution)/shard_map/all_gather | solution.py:144
  89.4 4.8 %all_gather.10 = bf16[192,256]{1,0:T(8,128)(2,1)S(1)} all-gather(bf16[96,256]{1,0:T(8,128)(2,1)S(1)} %slice.47), channel_id=1, replica_groups={{0,4},{8,12},{16,20},{24,28},{1,5},{9,13},{17,21},{25,29},{2,6},{10,14}..., dimensions={0}, use_global_device_ids=true | all-gather | bytes 147456 | tf_op jit(solution)/shard_map/all_gather | solution.py:46
  94.2 15.3 %all_gather.11 = bf16[768,256]{1,0:T(8,128)(2,1)S(1)} all-gather(bf16[192,256]{1,0:T(8,128)(2,1)S(1)} %all_gather.10), channel_id=1, replica_groups={{0,8,16,24},{4,12,20,28},{1,9,17,25},{5,13,21,29},{2,10,18,26},{6,14,22..., dimensions={0}, use_global_device_ids=true | all-gather | bytes 491520 | tf_op jit(solution)/shard_map/all_gather | solution.py:47
  110.0 0.5 convolution_convert_fusion
  110.7 1.0 collective-permute-start.9
  111.6 1.2 collective-permute-start.8
  112.8 2.4 %collective-permute-done.9 = bf16[24,2048]{1,0:T(8,128)(2,1)S(1)} collective-permute-done((bf16[24,2048]{1,0:T(8,128)(2,1)S(1)}, bf16[24,2048]{1,0:T(8,128)(2,1)S(1)}, u32[]{:S(2)}, u32[]{:S(2)}) %collective-permute-start.9) | collective-permute-done | bytes 98336 | tf_op jit(solution)/shard_map/ppermute | solution.py:57
  115.2 2.7 %collective-permute-done.8 = bf16[24,2048]{1,0:T(8,128)(2,1)S(1)} collective-permute-done((bf16[24,2048]{1,0:T(8,128)(2,1)S(1)}, bf16[24,2048]{1,0:T(8,128)(2,1)S(1)}, u32[]{:S(2)}, u32[]{:S(2)}) %collective-permute-start.8) | collective-permute-done | bytes 98336 | tf_op jit(solution)/shard_map/ppermute | solution.py:57
  118.0 1.1 fusion.17
  (42 shorter events, 2.1 us)
Async XLA Ops:
  0.0 110.0 %copy-start = (bf16[128,2048]{1,0:T(8,128)(2,1)S(1)}, bf16[128,2048]{1,0:T(8,128)(2,1)}, u32[]{:S(2)}) copy-start(bf16[128,2048]{1,0:T(8,128)(2,1)} %param.19) | copy-start | bytes 1572868
  1.1 17.5 %copy-start.1 = (bf16[1024,512]{1,0:T(8,128)(2,1)S(1)}, bf16[1024,512]{1,0:T(8,128)(2,1)}, u32[]{:S(2)}) copy-start(bf16[1024,512]{1,0:T(8,128)(2,1)} %param.14) | copy-start | bytes 3145732
  2.2 58.6 %collective-permute-start.2 = (bf16[192,2048]{1,0:T(8,128)(2,1)S(1)}, bf16[192,2048]{1,0:T(8,128)(2,1)}, u32[]{:S(2)}, u32[]{:S(2)}) collective-permute-start(bf16[192,2048]{1,0:T(8,128)(2,1)S(1)} %constant_dynamic-update-slice_fusion), channel_id=1, source_target_pairs={{0,1},{1,2},{2,3},{3,4},{4,5},{5,6},{6,7},{7,8},{8,9},{9,10},{10,1... | collective-permute-start | bytes 2359304 | tf_op jit(solution)/shard_map/ppermute | solution.py:19
  5.5 55.2 %collective-permute-start.1 = (bf16[192,2048]{1,0:T(8,128)(2,1)S(1)}, bf16[192,2048]{1,0:T(8,128)(2,1)}, u32[]{:S(2)}, u32[]{:S(2)}) collective-permute-start(bf16[192,2048]{1,0:T(8,128)(2,1)S(1)} %constant_dynamic-update-slice_fusion), channel_id=1, source_target_pairs={{0,2},{1,3},{2,4},{3,5},{4,6},{5,7},{6,8},{7,9},{8,10},{9,11},{10,... | collective-permute-start | bytes 2359304 | tf_op jit(solution)/shard_map/ppermute | solution.py:19
  10.0 54.3 %collective-permute-start.4 = (bf16[1024,512]{1,0:T(8,128)(2,1)}, bf16[1024,512]{1,0:T(8,128)(2,1)S(1)}, u32[]{:S(2)}, u32[]{:S(2)}) collective-permute-start(bf16[1024,512]{1,0:T(8,128)(2,1)} %param.14), channel_id=1, source_target_pairs={{0,2},{1,3},{2,0},{3,1},{4,6},{5,7},{6,4},{7,5},{8,10},{9,11},{10,... | collective-permute-start | bytes 3145736 | tf_op jit(solution)/shard_map/ppermute | solution.py:35
  10.6 57.0 %collective-permute-start.3 = (bf16[1024,512]{1,0:T(8,128)(2,1)}, bf16[1024,512]{1,0:T(8,128)(2,1)}, u32[]{:S(2)}, u32[]{:S(2)}) collective-permute-start(bf16[1024,512]{1,0:T(8,128)(2,1)} %param.14), channel_id=1, source_target_pairs={{0,1},{1,0},{2,3},{3,2},{4,5},{5,4},{6,7},{7,6},{8,9},{9,8},{10,11... | collective-permute-start | bytes 3145736 | tf_op jit(solution)/shard_map/ppermute | solution.py:24
  12.5 48.3 %collective-permute-start = (bf16[128,2048]{1,0:T(8,128)(2,1)}, bf16[128,2048]{1,0:T(8,128)(2,1)}, u32[]{:S(2)}, u32[]{:S(2)}) collective-permute-start(bf16[128,2048]{1,0:T(8,128)(2,1)} %slice.40), channel_id=1, source_target_pairs={{0,3},{1,4},{2,5},{3,6},{4,7},{5,8},{6,9},{7,10},{8,11},{9,12},{10... | collective-permute-start | bytes 1572872 | tf_op jit(solution)/shard_map/ppermute | solution.py:19
  62.5 1.0 copy-start.3
  64.3 6.8 %collective-permute-start.5 = (bf16[1024,512]{1,0:T(8,128)(2,1)S(1)}, bf16[1024,512]{1,0:T(8,128)(2,1)S(1)}, u32[]{:S(2)}, u32[]{:S(2)}) collective-permute-start(bf16[1024,512]{1,0:T(8,128)(2,1)S(1)} %collective-permute-done.4), channel_id=1, source_target_pairs={{0,1},{1,0},{2,3},{3,2},{4,5},{5,4},{6,7},{7,6},{8,9},{9,8},{10,11... | collective-permute-start | bytes 3145736 | tf_op jit(solution)/shard_map/ppermute | solution.py:24
  67.6 4.6 %copy-start.2 = (bf16[192,2048]{1,0:T(8,128)(2,1)S(1)}, bf16[192,2048]{1,0:T(8,128)(2,1)}, u32[]{:S(2)}) copy-start(bf16[192,2048]{1,0:T(8,128)(2,1)} %param.10) | copy-start | bytes 2359300
  72.2 7.4 %copy-start.4 = (f32[2048]{0:T(1024)S(1)}, f32[2048]{0:T(1024)}, u32[]{:S(2)}) copy-start(f32[2048]{0:T(1024)} %param.15) | copy-start | bytes 24580
  72.2 16.8 %copy-start.5 = (bf16[2048,128]{1,0:T(8,128)(2,1)S(1)}, bf16[2048,128]{1,0:T(8,128)(2,1)}, u32[]{:S(2)}) copy-start(bf16[2048,128]{1,0:T(8,128)(2,1)} %param.18) | copy-start | bytes 1572868
  72.2 16.8 %copy-start.6 = (bf16[2048,128]{1,0:T(8,128)(2,1)S(1)}, bf16[2048,128]{1,0:T(8,128)(2,1)}, u32[]{:S(2)}) copy-start(bf16[2048,128]{1,0:T(8,128)(2,1)} %param.17) | copy-start | bytes 1572868
  72.2 16.8 %copy-start.7 = (bf16[2048,128]{1,0:T(8,128)(2,1)S(1)}, bf16[2048,128]{1,0:T(8,128)(2,1)}, u32[]{:S(2)}) copy-start(bf16[2048,128]{1,0:T(8,128)(2,1)} %param.16) | copy-start | bytes 1572868
  76.2 3.3 %collective-permute-start.6 = (bf16[7,2048]{1,0:T(8,128)(2,1)S(1)}, bf16[7,2048]{1,0:T(8,128)(2,1)S(1)}, u32[]{:S(2)}, u32[]{:S(2)}) collective-permute-start(bf16[7,2048]{1,0:T(8,128)(2,1)S(1)} %slice.43), channel_id=1, source_target_pairs={{0,1},{1,2},{2,3},{3,4},{4,5},{5,6},{6,7},{7,8},{8,9},{9,10},{10,1... | collective-permute-start | bytes 86024 | tf_op jit(solution)/shard_map/ppermute | solution.py:19
  110.6 2.2 %collective-permute-start.7 = (bf16[24,2048]{1,0:T(8,128)(2,1)S(1)}, bf16[24,2048]{1,0:T(8,128)(2,1)S(1)}, u32[]{:S(2)}, u32[]{:S(2)}) collective-permute-start(bf16[24,2048]{1,0:T(8,128)(2,1)S(1)} %get-tuple-element.7), channel_id=1, source_target_pairs={{0,1},{1,0},{2,3},{3,2},{4,5},{5,4},{6,7},{7,6},{8,9},{9,8},{10,11... | collective-permute-start | bytes 294920 | tf_op jit(solution)/shard_map/ppermute | solution.py:57
  110.7 4.5 %collective-permute-start.9 = (bf16[24,2048]{1,0:T(8,128)(2,1)S(1)}, bf16[24,2048]{1,0:T(8,128)(2,1)S(1)}, u32[]{:S(2)}, u32[]{:S(2)}) collective-permute-start(bf16[24,2048]{1,0:T(8,128)(2,1)S(1)} %get-tuple-element.8), channel_id=1, source_target_pairs={{0,3},{1,2},{2,1},{3,0},{4,7},{5,6},{6,5},{7,4},{8,11},{9,10},{10,... | collective-permute-start | bytes 294920 | tf_op jit(solution)/shard_map/ppermute | solution.py:57
  111.6 6.3 %collective-permute-start.8 = (bf16[24,2048]{1,0:T(8,128)(2,1)S(1)}, bf16[24,2048]{1,0:T(8,128)(2,1)S(1)}, u32[]{:S(2)}, u32[]{:S(2)}) collective-permute-start(bf16[24,2048]{1,0:T(8,128)(2,1)S(1)} %get-tuple-element.9), channel_id=1, source_target_pairs={{0,2},{1,3},{2,0},{3,1},{4,6},{5,7},{6,4},{7,5},{8,10},{9,11},{10,... | collective-permute-start | bytes 294920 | tf_op jit(solution)/shard_map/ppermute | solution.py:57

commit v2 on v1

v2 whole, which is shorter than its diff:
```python
import functools
import math

import jax
import jax.numpy as jnp
from jax import lax
from jax.experimental import pallas as pl
from jax.experimental.pallas import tpu as pltpu
from jax.sharding import PartitionSpec as P

HE = 128
WIN = 512
POOL = 8
EXTRA = 16
BOTH = ("outer", "inner")

very_negative = -1e30


def on_ahead(block, distance):
    count = lax.axis_size(BOTH)
    return lax.ppermute(block, BOTH, [(i, i + distance) for i in range(count - distance)])


def swapped_cores(block):
    count = lax.axis_size("inner")
    return lax.ppermute(block, "inner", [(i, i ^ 1) for i in range(count)])


def outer_mate(outer, inner):
    return outer ^ (1 if (inner >> 1) % 2 == 0 else 2)


def mate_bit(outer, inner):
    return jnp.where((inner >> 1) % 2 == 0, outer % 2, (outer >> 1) % 2)


def shards_of_all(shard):
    count, blocks = lax.axis_size("inner"), lax.axis_size("outer")
    me, outer = lax.axis_index("inner"), lax.axis_index("outer")
    half = shard.shape[0] // 2
    mates = [
        (o * count + i, outer_mate(o, i) * count + i) for o in range(blocks) for i in range(count)
    ]
    fetched = []
    for hop in range(2, count, 2):
        wanted = mate_bit(outer, (me + hop) % count)
        part = lax.dynamic_slice_in_dim(shard, wanted * half, half, 0)
        near = lax.ppermute(part, "inner", [(i, (i + hop) % count) for i in range(count)])
        fetched.append((near, lax.ppermute(near, BOTH, mates)))
    pieces = [shard, swapped_cores(shard)]
    for near, far in fetched:
        pieces += [near, far, swapped_cores(near), swapped_cores(far)]
    return pieces


def outer_gather(block):
    count = lax.axis_size("outer")
    pairs = [[i, i + 1] for i in range(0, count, 2)]
    lines = [list(range(i, count, 2)) for i in range(2)]
    near = lax.all_gather(block, "outer", axis=0, tiled=True, axis_index_groups=pairs)
    return lax.all_gather(near, "outer", axis=0, tiled=True, axis_index_groups=lines)


def summed_pieces(block):
    count = lax.axis_size("inner")
    me = lax.axis_index("inner")
    parts = block.reshape(count, block.shape[0] // count, block.shape[1])
    own = lax.dynamic_index_in_dim(parts, me, 0, keepdims=False).astype(jnp.float32)
    for hop in range(1, count):
        piece = lax.dynamic_index_in_dim(parts, me ^ hop, 0, keepdims=False)
        own = own + lax.ppermute(piece, "inner", [(i, i ^ hop) for i in range(count)]).astype(
            jnp.float32
        )
    return own


def attention_kernel(takes, query, key, value, mate, *refs):
    halos = refs[: len(takes)]
    mine_out, send_out, q_all, k_all, v_all, bias, sems = refs[len(takes) :]
    rows = query.shape[0]
    width = q_all.shape[1]
    core = lax.axis_index("inner") % 2
    chip = (lax.axis_index("outer") * lax.axis_size("inner") + lax.axis_index("inner")) // 2
    halo = sum(takes)
    copies = []

    def place(source, target):
        copy = pltpu.make_async_copy(source, target, sems.at[len(copies)])
        copy.start()
        copies.append(copy)

    own = pl.multiple_of(core * rows, 16)
    other = pl.multiple_of((1 - core) * rows, 16)
    columns = pl.ds(pl.multiple_of(core * width, 128), width)
    place(query.at[:, columns], q_all.at[pl.ds(EXTRA + own, rows)])
    place(key.at[:, columns], k_all.at[pl.ds(halo + own, rows)])
    place(value.at[:, columns], v_all.at[pl.ds(halo + own, rows)])
    place(mate.at[:, pl.ds(0, width)], q_all.at[pl.ds(EXTRA + other, rows)])
    place(mate.at[:, pl.ds(width, width)], k_all.at[pl.ds(halo + other, rows)])
    place(mate.at[:, pl.ds(2 * width, width)], v_all.at[pl.ds(halo + other, rows)])
    place(halos[0].at[pl.ds(takes[0], EXTRA), pl.ds(0, width)], q_all.at[pl.ds(0, EXTRA)])
    start = halo
    for take, ref in zip(takes, halos):
        start -= take
        place(ref.at[pl.ds(0, take), pl.ds(0, width)], k_all.at[pl.ds(start, take)])
        place(ref.at[pl.ds(0, take), pl.ds(width, width)], v_all.at[pl.ds(start, take)])

    count, span = mine_out.shape[0], halo + rows
    row = lax.broadcasted_iota(jnp.int32, (count, span), 0) - EXTRA
    col = lax.broadcasted_iota(jnp.int32, (count, span), 1) - halo
    gap = row - col
    near = (gap >= 0) & (gap < WIN)
    scale = 1.0 / math.sqrt(HE)
    for copy in copies:
        copy.wait()
    for which, out in ((1 - core, send_out), (core, mine_out)):
        first = pl.multiple_of(which * rows, 16)
        bias[...] = jnp.where(near & (col + chip * 2 * rows + first >= 0), 0.0, very_negative)
        for head in range(width // HE):
            lanes = pl.ds(head * HE, HE)
            scores = lax.dot_general(
                q_all[pl.ds(first, count), lanes],
                k_all[pl.ds(first, span), lanes],
                (((1,), (1,)), ((), ())),
                preferred_element_type=jnp.float32,
            )
            masked = scores * scale + bias[...]
            top = jnp.max(masked, axis=-1, keepdims=True)
            weights = jnp.exp(masked - top)
            total = jnp.sum(weights, axis=-1, keepdims=True)
            summed = jnp.dot(
                weights.astype(jnp.bfloat16),
                v_all[pl.ds(first, span), lanes],
                preferred_element_type=jnp.float32,
            )
            out[:, lanes] = (summed / total).astype(jnp.bfloat16)


def fine_attention(fine_query, fine_key, fine_value):
    rows, full = fine_query.shape
    width = full // 2
    core = lax.axis_index("inner") % 2
    away = (1 - core) * width
    kept = core * width
    parts = (fine_query, fine_key, fine_value)
    mate = swapped_cores(
        jnp.concatenate([lax.dynamic_slice_in_dim(a, away, width, 1) for a in parts], axis=1)
    )
    mine = jnp.concatenate([lax.dynamic_slice_in_dim(a, kept, width, 1) for a in parts], axis=1)
    low = jnp.where(core == 0, mine, mate)
    high = jnp.where(core == 0, mate, mine)
    left = -(-(WIN - 1 + EXTRA) // 16) * 16
    takes = []
    while left > 0:
        takes.append(min(left, 2 * rows))
        left -= takes[-1]
    chip_kv = jnp.concatenate([low[:, width:], high[:, width:]], axis=0)
    halos = []
    for at, take in enumerate(takes):
        block = chip_kv[2 * rows - take :]
        if at == 0:
            edge = jnp.pad(high[rows - EXTRA :, :width], ((0, 0), (0, width)))
            block = jnp.concatenate([block, edge], axis=0)
        halos.append(on_ahead(block, 2 * (at + 1)))
    count, halo = rows + EXTRA, sum(takes)
    anywhere = pl.BlockSpec(memory_space=pl.ANY)
    out = jax.ShapeDtypeStruct((count, width), jnp.bfloat16)
    pairs = 4 * (width // HE) * count * (halo + rows)
    return pl.pallas_call(
        functools.partial(attention_kernel, tuple(takes)),
        out_shape=(out, out),
        in_specs=[anywhere] * (4 + len(takes)),
        out_specs=(pl.BlockSpec(memory_space=pltpu.VMEM),) * 2,
        scratch_shapes=[
            pltpu.VMEM((2 * rows + EXTRA, width), jnp.bfloat16),
            pltpu.VMEM((2 * rows + halo, width), jnp.bfloat16),
            pltpu.VMEM((2 * rows + halo, width), jnp.bfloat16),
            pltpu.VMEM((count, halo + rows), jnp.float32),
            pltpu.SemaphoreType.DMA((7 + 2 * len(takes),)),
        ],
        compiler_params=pltpu.CompilerParams(vmem_limit_bytes=24 * 1024 * 1024),
        cost_estimate=pl.CostEstimate(
            flops=2 * pairs * HE, bytes_accessed=6 * rows * full, transcendentals=pairs // 2
        ),
        name="fine_attention",
    )(fine_query, fine_key, fine_value, mate, *halos)


def state_kernel(counts, mix_mine, mix_mate, stream, edge, gain, *refs):
    pieces, refs = refs[: counts[0]], refs[counts[0] :]
    state_out, pooled_out, normed_out, mix, weights, wide, sems = refs
    rows, model_width = stream.shape
    devices = lax.axis_size("inner")
    shard = model_width // devices
    depth, half = weights.shape[1], weights.shape[1] // 2
    me, outer = lax.axis_index("inner"), lax.axis_index("outer")
    core = me % 2
    bit = jnp.where((me // 2) % 2 == 0, outer % 2, (outer // 2) % 2)
    first_half = pl.ds(pl.multiple_of(bit * half, 16), half)
    second_half = pl.ds(pl.multiple_of((1 - bit) * half, 16), half)
    slots = [[(pieces[0], None)], [(pieces[1], None)]]
    owners = [me, me + 1 - 2 * core]
    for hop in range(2, devices, 2):
        near, far, near_mate, far_mate = pieces[2 * hop - 2 : 2 * hop + 2]
        owner = lax.rem(me - hop + devices, devices)
        slots += [
            [(near, first_half), (far, second_half)],
            [(near_mate, first_half), (far_mate, second_half)],
        ]
        owners += [owner, owner + 1 - 2 * core]
    copies = []
    for slot, parts in enumerate(slots):
        group = []
        for at, (ref, where) in enumerate(parts):
            target = weights.at[slot] if where is None else weights.at[slot, where]
            group.append(pltpu.make_async_copy(ref, target, sems.at[2 * slot + at]))
            group[-1].start()
        copies.append(group)
    width = depth // 2
    mix[:, pl.ds(pl.multiple_of(core * width, 128), width)] = mix_mine[...]
    mix[:, pl.ds(pl.multiple_of((1 - core) * width, 128), width)] = mix_mate[...]
    started = jnp.where(me + outer > 0, 1.0, 0.0)
    groups = rows // POOL
    moment = jnp.zeros((groups, 1), jnp.float32)
    for slot, owner in enumerate(owners):
        for copy in copies[slot]:
            copy.wait()
        columns = pl.ds(pl.multiple_of(owner * shard, 128), shard)
        projected = jnp.dot(mix[...], weights[slot], preferred_element_type=jnp.float32)
        before = (edge[:, columns].astype(jnp.float32) + projected[:EXTRA]).astype(jnp.bfloat16)
        state = (stream[:, columns].astype(jnp.float32) + projected[EXTRA:]).astype(jnp.bfloat16)
        state_out[:, columns] = state
        before = before[EXTRA - POOL :].astype(jnp.float32) * started
        cells = jnp.concatenate([before, state.astype(jnp.float32)], axis=0)
        cells = cells.reshape(groups + 1, POOL, shard)
        tail = jnp.where(lax.broadcasted_iota(jnp.int32, cells.shape, 1) > 0, cells, 0.0)
        tail = jnp.sum(tail, axis=1)
        head = jnp.where(lax.broadcasted_iota(jnp.int32, cells.shape, 1) > 0, 0.0, cells)
        head = jnp.sum(head, axis=1)
        pooled = ((tail[:groups] + head[1:]) / POOL).astype(jnp.bfloat16)
        pooled_out[:, columns] = pooled
        pooled = pooled.astype(jnp.float32)
        wide[:, columns] = pooled
        moment = moment + jnp.sum(pooled * pooled, axis=-1, keepdims=True)
    factor = lax.rsqrt(moment / model_width + 1e-06)
    normed_out[...] = (wide[...] * factor * gain[...]).astype(jnp.bfloat16)


def fine_state_of(mixes, stream, edge, gain, pieces):
    rows, model_width = stream.shape
    devices = lax.axis_size("inner")
    depth, shard = pieces[0].shape
    groups = rows // POOL
    anywhere = pl.BlockSpec(memory_space=pl.ANY)
    inside = pl.BlockSpec(memory_space=pltpu.VMEM)
    return pl.pallas_call(
        functools.partial(state_kernel, (len(pieces),)),
        out_shape=(
            jax.ShapeDtypeStruct((rows, model_width), jnp.bfloat16),
            jax.ShapeDtypeStruct((groups, model_width), jnp.bfloat16),
            jax.ShapeDtypeStruct((groups, model_width), jnp.bfloat16),
        ),
        in_specs=[inside] * 5 + [anywhere] * len(pieces),
        out_specs=(inside,) * 3,
        scratch_shapes=[
            pltpu.VMEM((rows + EXTRA, depth), jnp.bfloat16),
            pltpu.VMEM((devices, depth, shard), jnp.bfloat16),
            pltpu.VMEM((groups, model_width), jnp.float32),
            pltpu.SemaphoreType.DMA((2 * devices,)),
        ],
        compiler_params=pltpu.CompilerParams(vmem_limit_bytes=24 * 1024 * 1024),
        cost_estimate=pl.CostEstimate(
            flops=2 * (rows + EXTRA) * depth * model_width,
            bytes_accessed=2 * depth * model_width + 4 * rows * model_width,
            transcendentals=groups,
        ),
        name="fine_state",
    )(*mixes, stream, edge, gain.reshape(1, model_width), *pieces)


def on_device(
    fine_input,
    fine_query,
    fine_key,
    fine_value,
    w_fine_out,
    norm_gain,
    w_query,
    w_key,
    w_value,
    w_coarse_out,
):
    tok_rows, model_width = fine_input.shape
    score_scale = 1.0 / math.sqrt(HE)
    edge = on_ahead(fine_input[tok_rows - EXTRA :], 1)
    pieces = shards_of_all(w_fine_out)
    mix_mine, mix_send = fine_attention(fine_query, fine_key, fine_value)
    mixes = (mix_mine, swapped_cores(mix_send))
    fine_state, pooled, normed = fine_state_of(mixes, fine_input, edge, norm_gain, pieces)
    pooled_wide = pooled.astype(jnp.float32)
    local_heads = w_query.shape[1] // HE
    head_width = local_heads * HE
    joined_weights = jnp.concatenate([w_query, w_key, w_value], axis=1)
    projections = jnp.dot(
        lax.all_gather(normed, "inner", axis=0, tiled=True),
        joined_weights,
        preferred_element_type=jnp.float32,
    ).astype(jnp.bfloat16)
    group_len = projections.shape[0]
    coarse_query = projections[:, :head_width].reshape(group_len, local_heads, HE)
    outer_index = lax.axis_index("outer")
    query_pos = outer_index * group_len + jnp.arange(group_len, dtype=jnp.int32)
    gathered = outer_gather(projections[:, head_width:])
    count = gathered.shape[0]
    block_keys = gathered[:, :head_width].reshape(count, local_heads, HE)
    block_values = gathered[:, head_width:].reshape(count, local_heads, HE)
    block_scores = (
        jnp.einsum("qhe,khe->hqk", coarse_query, block_keys, preferred_element_type=jnp.float32)
        * score_scale
    )
    key_pos = jnp.arange(count, dtype=jnp.int32)
    visible = (key_pos[None, :] <= query_pos[:, None])[None]
    block_masked = jnp.where(visible, block_scores, very_negative)
    new_max = jnp.max(block_masked, axis=-1)
    block_exp = jnp.where(visible, jnp.exp(block_scores - new_max[:, :, None]), 0.0)
    new_sum = jnp.sum(block_exp, axis=-1)
    contrib = jnp.einsum(
        "hqk,khe->hqe",
        block_exp.astype(jnp.bfloat16),
        block_values,
        preferred_element_type=jnp.float32,
    )
    coarse_mix = (
        jnp.transpose(contrib / new_sum[:, :, None], (1, 0, 2))
        .reshape(group_len, head_width)
        .astype(jnp.bfloat16)
    )
    head_total = summed_pieces(
        jnp.dot(coarse_mix, w_coarse_out, preferred_element_type=jnp.float32).astype(jnp.bfloat16)
    )
    coarse_out = (pooled_wide + head_total).astype(jnp.bfloat16)
    fine_groups = fine_state.reshape(tok_rows // POOL, POOL, model_width).astype(jnp.float32)
    lifted = fine_groups + coarse_out.astype(jnp.float32)[:, None, :]
    return lifted.reshape(tok_rows, model_width).astype(jnp.bfloat16)


def solution(mesh):
    placed = (
        P(("outer", "inner"), None),
        P(("outer", "inner"), None),
        P(("outer", "inner"), None),
        P(("outer", "inner"), None),
        P(None, "inner"),
        P(),
        P(None, "inner"),
        P(None, "inner"),
        P(None, "inner"),
        P("inner", None),
    )
    return jax.shard_map(
        on_device,
        mesh=mesh,
        in_specs=placed,
        out_specs=P(("outer", "inner"), None),
        check_vma=False,
    )
```

time: 119 us -> 112 us (0.941)
  waiting for transfers between devices: 46.7 us -> 28.1 us
  starting transfers between devices: 17.8 us -> 32.1 us
  Pallas kernels: 0 us -> 7.91 us
  local copies, waits for them, and re-layouts: 12.3 us -> 7.25 us
  matrix products: 6.15 us -> 1.2 us
  other arithmetic: 6.57 us -> 3.59 us
  blocking collectives: 29.3 us -> 31.2 us
    ppermute x5, waiting for transfers between devices: 41.6 us -> 23.9 us  [the longest x1 10.3 us: shards_of_all(): fetched.append((near, lax.ppermute(near, BOTH, mates)))]
    ppermute x5, starting transfers between devices: 14.4 us -> 29.5 us  [the longest x1 19.3 us: shards_of_all(): fetched.append((near, lax.ppermute(near, BOTH, mates)))]
    pallas_call x0 -> x2, Pallas kernels: none -> 7.91 us  [the longest x1 4.1 us: fine_attention(): pl.pallas_call(functools.partial(attention_kernel, tuple(takes)), out_sha...]
    dynamic_update_slice x4 -> x0, local copies, waits for them, and re-layouts: 5.72 us -> none  [the longest x2 3.5 us: columns_of_all(): lax.dynamic_update_slice(joined, swapped_cores(near), (0, (owner ^ 1) * w...]
    dot_general x3 -> x0, matrix products: 4.94 us -> none  [the longest x1 3.36 us: on_device(): jnp.dot(fine_mix, columns_of_all(w_fine_out), preferred_element_type=jnp....]
    dynamic_slice x0 -> x3, local copies, waits for them, and re-layouts: none -> 3.53 us  [the longest x2 2.68 us: fine_attention(): lax.dynamic_slice_in_dim(a, kept, width, 1)]
    broadcast_in_dim x1 -> x0, local copies, waits for them, and re-layouts: 2.46 us -> none  [columns_of_all(): joined = jnp.zeros((rows, count * width), shard.dtype)]
    sub x2 -> x0, other arithmetic: 2.43 us -> none  [the longest x1 2.43 us: on_device(): exp_weights = jnp.where(allowed[None], jnp.exp(scores - row_max), 0.0)]
  transfers between devices with their start and end apart: 10 -> 13, of which waited for: 4 -> 6; matrix products, arithmetic and copies ran while one was open for 12% -> 3% of each run, Pallas kernels for 0% -> 4%
where the time goes in v2:
time: 112 us
  starting transfers between devices  32.1 us (29%)
  blocking collectives  31.2 us (28%)
  waiting for transfers between devices  28.1 us (25%)
  Pallas kernels  7.91 us (7%)
  local copies, waits for them, and re-layouts  7.25 us (6%)
  other arithmetic  3.59 us (3%)
  matrix products  1.2 us (1%)
    ppermute x1, starting transfers between devices, shards_of_all(): fetched.append((near, lax.ppermute(near, BOTH, mates)))  19.3 us
    all_gather x1, blocking collectives, outer_gather(): lax.all_gather(near, 'outer', axis=0, tiled=True, axis_index_groups=lines)  16.5 us
    ppermute x1, waiting for transfers between devices, shards_of_all(): fetched.append((near, lax.ppermute(near, BOTH, mates)))  10.3 us
    all_gather x1, blocking collectives, on_device(): lax.all_gather(normed, 'inner', axis=0, tiled=True)  8.46 us
    ppermute x1, waiting for transfers between devices, shards_of_all(): lax.ppermute(part, 'inner', [(i, (i + hop) % count) for i in range(count)])  7.81 us
    ppermute x3, starting transfers between devices, on_ahead(): lax.ppermute(block, BOTH, [(i, i + distance) for i in range(count - dista...  7.77 us
    all_gather x1, blocking collectives, outer_gather(): lax.all_gather(block, 'outer', axis=0, tiled=True, axis_index_groups=pairs)  6.25 us
    ppermute x3, waiting for transfers between devices, on_ahead(): lax.ppermute(block, BOTH, [(i, i + distance) for i in range(count - dista...  5.85 us
  transfers between devices with their start and end apart: 13, of which 6 were waited for; matrix products, arithmetic and copies ran while one was open for 3% of the time, Pallas kernels for 4%

profile of v2, /device:TPU:0, one launch (start us, length us, event | category | flops | bytes accessed | tf_op | source)
XLA Modules:
  0.0 111.7 jit_solution(3856258800464332674)
XLA Ops:
  0.0 1.8 %constant_dynamic-slice_fusion.3 = (bf16[192,512]{1,0:T(8,128)(2,1)}, bf16[192,512]{1,0:T(8,128)(2,1)S(1)}) fusion(bf16[192,1024]{1,0:T(8,128)(2,1)} %query.1, s32[]{:T(128)S(6)} %select_n.76, s32[]{:T(128)S(6)} %select_n.74), kind=kLoop, calls=%fused_computation.44 | loop fusion | bytes 786440 | tf_op jit(solution)/shard_map/dynamic_slice | solution.py:150
  1.9 0.8 constant_dynamic-slice_fusion.1
  2.7 0.9 pad_maximum_fusion
  3.5 0.5 collective-permute-start
  4.1 0.9 constant_dynamic-slice_fusion
  4.9 2.5 %collective-permute-start.6 = (bf16[512,512]{1,0:T(8,128)(2,1)}, bf16[512,512]{1,0:T(8,128)(2,1)S(1)}, u32[]{:S(2)}, u32[]{:S(2)}) collective-permute-start(bf16[512,512]{1,0:T(8,128)(2,1)} %constant_dynamic-slice_fusion), channel_id=1, source_target_pairs={{0,2},{1,3},{2,0},{3,1},{4,6},{5,7},{6,4},{7,5},{8,10},{9,11},{10,... | collective-permute-start | bytes 1572872 | tf_op jit(solution)/shard_map/ppermute | solution.py:49
  7.4 1.3 %pad_maximum_fusion.1 = (bf16[192,1536]{1,0:T(8,128)(2,1)S(1)}, bf16[192,1536]{1,0:T(8,128)(2,1)S(1)}) fusion(bf16[192,512]{1,0:T(8,128)(2,1)} %get-tuple-element.24, bf16[192,512]{1,0:T(8,128)(2,1)} %get-tuple-element.29, bf16[192,512]{1,0:T(8,128)(2,1)} %get-tuple-element.20, bf16[192,1536]{1,0:T(8,128)(2,1)S(1)} %collective-permute-done.mate, pred[]{:T(512)S(6)} %eq.13), kind=kLoop, calls=%fused_computation.17 | loop fusion | flops 2064384 | bytes 2359297 | tf_op jit(solution)/shard_map/concatenate | solution.py:150
  8.9 3.4 %collective-permute-start.1 = (bf16[400,1024]{1,0:T(8,128)(2,1)S(1)}, bf16[400,1024]{1,0:T(8,128)(2,1)S(1)}, u32[]{:S(2)}, u32[]{:S(2)}) collective-permute-start(bf16[400,1024]{1,0:T(8,128)(2,1)S(1)} %fusion.12), channel_id=1, source_target_pairs={{0,2},{1,3},{2,4},{3,5},{4,6},{5,7},{6,8},{7,9},{8,10},{9,11},{10,... | collective-permute-start | bytes 2457608 | tf_op jit(solution)/shard_map/ppermute | solution.py:22
  12.4 7.8 %collective-permute-done.6.refs_2_ = bf16[512,512]{1,0:T(8,128)(2,1)S(1)} collective-permute-done((bf16[512,512]{1,0:T(8,128)(2,1)}, bf16[512,512]{1,0:T(8,128)(2,1)S(1)}, u32[]{:S(2)}, u32[]{:S(2)}) %collective-permute-start.6) | collective-permute-done | bytes 524320 | tf_op jit(solution)/shard_map/ppermute | solution.py:49
  20.2 19.3 %collective-permute-start.7 = (bf16[512,512]{1,0:T(8,128)(2,1)S(1)}, bf16[512,512]{1,0:T(8,128)(2,1)}, u32[]{:S(2)}, u32[]{:S(2)}) collective-permute-start(bf16[512,512]{1,0:T(8,128)(2,1)S(1)} %collective-permute-done.6.refs_2_), channel_id=1, source_target_pairs={{0,4},{1,5},{2,10},{3,11},{4,0},{5,1},{6,14},{7,15},{8,12},{9,13},... | collective-permute-start | bytes 1572872 | tf_op jit(solution)/shard_map/ppermute | solution.py:50
  39.5 1.9 %collective-permute-start.2 = (bf16[144,1024]{1,0:T(8,128)(2,1)S(1)}, bf16[144,1024]{1,0:T(8,128)(2,1)S(1)}, u32[]{:S(2)}, u32[]{:S(2)}) collective-permute-start(bf16[144,1024]{1,0:T(8,128)(2,1)S(1)} %slice.41), channel_id=1, source_target_pairs={{0,4},{1,5},{2,6},{3,7},{4,8},{5,9},{6,10},{7,11},{8,12},{9,13},{1... | collective-permute-start | bytes 884744 | tf_op jit(solution)/shard_map/ppermute | solution.py:22
  41.6 10.3 %collective-permute-done.7.refs_3_ = bf16[512,512]{1,0:T(8,128)(2,1)} collective-permute-done((bf16[512,512]{1,0:T(8,128)(2,1)S(1)}, bf16[512,512]{1,0:T(8,128)(2,1)}, u32[]{:S(2)}, u32[]{:S(2)}) %collective-permute-start.7) | collective-permute-done | bytes 524320 | tf_op jit(solution)/shard_map/ppermute | solution.py:50
  51.8 5.0 %collective-permute-done.2.refs_1_ = bf16[144,1024]{1,0:T(8,128)(2,1)S(1)} collective-permute-done((bf16[144,1024]{1,0:T(8,128)(2,1)S(1)}, bf16[144,1024]{1,0:T(8,128)(2,1)S(1)}, u32[]{:S(2)}, u32[]{:S(2)}) %collective-permute-start.2) | collective-permute-done | bytes 294944 | tf_op jit(solution)/shard_map/ppermute | solution.py:22
  56.8 4.1 %fine_attention.1 = (bf16[208,512]{1,0:T(8,128)(2,1)S(1)}, bf16[208,512]{1,0:T(8,128)(2,1)}) custom-call(bf16[192,1024]{1,0:T(8,128)(2,1)S(1)} %copy-done.2, bf16[192,1024]{1,0:T(8,128)(2,1)S(1)} %copy-done.3, bf16[192,1024]{1,0:T(8,128)(2,1)S(1)} %copy-done.4, bf16[192,1536]{1,0:T(8,128)(2,1)S(1)} %collective-permute-done.mate, ...), custom_call_target="tpu_custom_call" | custom-call | flops 613416960 | bytes 1179648 | tf_op jit(solution)/shard_map/fine_attention/pallas_call | solution.py:170
  61.0 0.7 copy-done.6
  61.6 0.8 slice.32
  62.5 2.4 %collective-permute-start.4 = (bf16[16,2048]{1,0:T(8,128)(2,1)S(1)}, bf16[16,2048]{1,0:T(8,128)(2,1)S(1)}, u32[]{:S(2)}, u32[]{:S(2)}) collective-permute-start(bf16[16,2048]{1,0:T(8,128)(2,1)S(1)} %slice.32), channel_id=1, source_target_pairs={{0,1},{1,2},{2,3},{3,4},{4,5},{5,6},{6,7},{7,8},{8,9},{9,10},{10,1... | collective-permute-start | bytes 196616 | tf_op jit(solution)/shard_map/ppermute | solution.py:22
  64.9 0.8 collective-permute-done.4.edge
  65.8 1.1 %copy-done.5 = bf16[192,2048]{1,0:T(8,128)(2,1)S(1)} copy-done((bf16[192,2048]{1,0:T(8,128)(2,1)S(1)}, bf16[192,2048]{1,0:T(8,128)(2,1)}, u32[]{:S(2)}) %copy-start.5) | copy-done | bytes 786456
  66.9 0.9 copy-done.7
  67.9 3.8 %fine_state.1 = (bf16[192,2048]{1,0:T(8,128)(2,1)S(1)}, bf16[24,2048]{1,0:T(8,128)(2,1)S(1)}, bf16[24,2048]{1,0:T(8,128)(2,1)S(1)}) custom-call(bf16[208,512]{1,0:T(8,128)(2,1)S(1)} %copy-done.7, bf16[208,512]{1,0:T(8,128)(2,1)S(1)} %collective-permute-done.3.mix_mate, bf16[192,2048]{1,0:T(8,128)(2,1)S(1)} %copy-done.5, ...), custom_call_target="tpu_custom_call" | custom-call | flops 872415232 | bytes 5767168 | tf_op jit(solution)/shard_map/fine_state/pallas_call | solution.py:257
  71.7 8.5 %all_gather.9 = bf16[96,2048]{1,0:T(8,128)(2,1)S(1)} all-gather(bf16[24,2048]{1,0:T(8,128)(2,1)S(1)} %get-tuple-element.14), channel_id=1, replica_groups=mesh['outer'=8,'inner'=4] {'inner'}, dimensions={0}, use_global_device_ids=true | all-gather | bytes 491520 | tf_op jit(solution)/shard_map/all_gather | solution.py:306
  80.2 0.4 fusion.8
  80.6 6.2 %all_gather.10 = bf16[192,256]{1,0:T(8,128)(2,1)S(1)} all-gather(bf16[96,256]{1,0:T(8,128)(2,1)S(1)} %slice.43), channel_id=1, replica_groups={{0,4},{8,12},{16,20},{24,28},{1,5},{9,13},{17,21},{25,29},{2,6},{10,14}..., dimensions={0}, use_global_device_ids=true | all-gather | bytes 147456 | tf_op jit(solution)/shard_map/all_gather | solution.py:61
  86.8 16.5 %all_gather.11 = bf16[768,256]{1,0:T(8,128)(2,1)S(1)} all-gather(bf16[192,256]{1,0:T(8,128)(2,1)S(1)} %all_gather.10), channel_id=1, replica_groups={{0,8,16,24},{4,12,20,28},{1,9,17,25},{5,13,21,29},{2,10,18,26},{6,14,22..., dimensions={0}, use_global_device_ids=true | all-gather | bytes 491520 | tf_op jit(solution)/shard_map/all_gather | solution.py:62
  103.4 0.3 select_reduce_fusion
  103.9 0.5 convolution_convert_fusion
  104.5 0.9 collective-permute-start.11
  105.4 0.9 collective-permute-start.10
  106.4 3.2 %collective-permute-done.12 = bf16[24,2048]{1,0:T(8,128)(2,1)S(1)} collective-permute-done((bf16[24,2048]{1,0:T(8,128)(2,1)S(1)}, bf16[24,2048]{1,0:T(8,128)(2,1)S(1)}, u32[]{:S(2)}, u32[]{:S(2)}) %collective-permute-start.12) | collective-permute-done | bytes 98336 | tf_op jit(solution)/shard_map/ppermute | solution.py:72
  109.6 0.9 collective-permute-done.11
  110.6 1.1 fusion.7
  (43 shorter events, 0.8 us)
Async XLA Ops:
  0.0 103.9 %copy-start = (bf16[128,2048]{1,0:T(8,128)(2,1)S(1)}, bf16[128,2048]{1,0:T(8,128)(2,1)}, u32[]{:S(2)}) copy-start(bf16[128,2048]{1,0:T(8,128)(2,1)} %param.19) | copy-start | bytes 1572868
  0.0 1.9 %copy-start.3 = (bf16[192,1024]{1,0:T(8,128)(2,1)S(1)}, bf16[192,1024]{1,0:T(8,128)(2,1)}, u32[]{:S(2)}) copy-start(bf16[192,1024]{1,0:T(8,128)(2,1)} %key.1) | copy-start | bytes 1179652
  0.0 1.9 %copy-start.4 = (bf16[192,1024]{1,0:T(8,128)(2,1)S(1)}, bf16[192,1024]{1,0:T(8,128)(2,1)}, u32[]{:S(2)}) copy-start(bf16[192,1024]{1,0:T(8,128)(2,1)} %value.1) | copy-start | bytes 1179652
  1.9 2.2 %copy-start.1 = (bf16[1024,512]{1,0:T(8,128)(2,1)S(1)}, bf16[1024,512]{1,0:T(8,128)(2,1)}, u32[]{:S(2)}) copy-start(bf16[1024,512]{1,0:T(8,128)(2,1)} %refs_0_.1) | copy-start | bytes 3145732
  3.5 3.9 %collective-permute-start = (bf16[192,1536]{1,0:T(8,128)(2,1)}, bf16[192,1536]{1,0:T(8,128)(2,1)S(1)}, u32[]{:S(2)}, u32[]{:S(2)}) collective-permute-start(bf16[192,1536]{1,0:T(8,128)(2,1)} %pad_maximum_fusion), channel_id=1, source_target_pairs={{0,1},{1,0},{2,3},{3,2},{4,5},{5,4},{6,7},{7,6},{8,9},{9,8},{10,11... | collective-permute-start | bytes 1769480 | tf_op jit(solution)/shard_map/ppermute | solution.py:27
  4.9 15.3 %collective-permute-start.6 = (bf16[512,512]{1,0:T(8,128)(2,1)}, bf16[512,512]{1,0:T(8,128)(2,1)S(1)}, u32[]{:S(2)}, u32[]{:S(2)}) collective-permute-start(bf16[512,512]{1,0:T(8,128)(2,1)} %constant_dynamic-slice_fusion), channel_id=1, source_target_pairs={{0,2},{1,3},{2,0},{3,1},{4,6},{5,7},{6,4},{7,5},{8,10},{9,11},{10,... | collective-permute-start | bytes 1572872 | tf_op jit(solution)/shard_map/ppermute | solution.py:49
  8.8 48.0 %copy-start.2 = (bf16[192,1024]{1,0:T(8,128)(2,1)S(1)}, bf16[192,1024]{1,0:T(8,128)(2,1)}, u32[]{:S(2)}) copy-start(bf16[192,1024]{1,0:T(8,128)(2,1)} %query.1) | copy-start | bytes 1179652
  8.9 47.9 %collective-permute-start.1 = (bf16[400,1024]{1,0:T(8,128)(2,1)S(1)}, bf16[400,1024]{1,0:T(8,128)(2,1)S(1)}, u32[]{:S(2)}, u32[]{:S(2)}) collective-permute-start(bf16[400,1024]{1,0:T(8,128)(2,1)S(1)} %fusion.12), channel_id=1, source_target_pairs={{0,2},{1,3},{2,4},{3,5},{4,6},{5,7},{6,8},{7,9},{8,10},{9,11},{10,... | collective-permute-start | bytes 2457608 | tf_op jit(solution)/shard_map/ppermute | solution.py:22
  12.3 53.4 %collective-permute-start.5 = (bf16[1024,512]{1,0:T(8,128)(2,1)S(1)}, bf16[1024,512]{1,0:T(8,128)(2,1)}, u32[]{:S(2)}, u32[]{:S(2)}) collective-permute-start(bf16[1024,512]{1,0:T(8,128)(2,1)S(1)} %copy-done.1), channel_id=1, source_target_pairs={{0,1},{1,0},{2,3},{3,2},{4,5},{5,4},{6,7},{7,6},{8,9},{9,8},{10,11... | collective-permute-start | bytes 3145736 | tf_op jit(solution)/shard_map/ppermute | solution.py:27
  20.2 31.6 %collective-permute-start.7 = (bf16[512,512]{1,0:T(8,128)(2,1)S(1)}, bf16[512,512]{1,0:T(8,128)(2,1)}, u32[]{:S(2)}, u32[]{:S(2)}) collective-permute-start(bf16[512,512]{1,0:T(8,128)(2,1)S(1)} %collective-permute-done.6.refs_2_), channel_id=1, source_target_pairs={{0,4},{1,5},{2,10},{3,11},{4,0},{5,1},{6,14},{7,15},{8,12},{9,13},... | collective-permute-start | bytes 1572872 | tf_op jit(solution)/shard_map/ppermute | solution.py:50
  39.5 26.3 %copy-start.8 = (f32[2048]{0:T(1024)S(1)}, f32[2048]{0:T(1024)}, u32[]{:S(2)}) copy-start(f32[2048]{0:T(1024)} %param.15) | copy-start | bytes 24580
  39.5 17.3 %collective-permute-start.2 = (bf16[144,1024]{1,0:T(8,128)(2,1)S(1)}, bf16[144,1024]{1,0:T(8,128)(2,1)S(1)}, u32[]{:S(2)}, u32[]{:S(2)}) collective-permute-start(bf16[144,1024]{1,0:T(8,128)(2,1)S(1)} %slice.41), channel_id=1, source_target_pairs={{0,4},{1,5},{2,6},{3,7},{4,8},{5,9},{6,10},{7,11},{8,12},{9,13},{1... | collective-permute-start | bytes 884744 | tf_op jit(solution)/shard_map/ppermute | solution.py:22
  41.5 24.3 %collective-permute-start.8 = (bf16[512,512]{1,0:T(8,128)(2,1)S(1)}, bf16[512,512]{1,0:T(8,128)(2,1)}, u32[]{:S(2)}, u32[]{:S(2)}) collective-permute-start(bf16[512,512]{1,0:T(8,128)(2,1)S(1)} %collective-permute-done.6.refs_2_), channel_id=1, source_target_pairs={{0,1},{1,0},{2,3},{3,2},{4,5},{5,4},{6,7},{7,6},{8,9},{9,8},{10,11... | collective-permute-start | bytes 1572872 | tf_op jit(solution)/shard_map/ppermute | solution.py:27
  51.8 14.0 %collective-permute-start.9 = (bf16[512,512]{1,0:T(8,128)(2,1)}, bf16[512,512]{1,0:T(8,128)(2,1)}, u32[]{:S(2)}, u32[]{:S(2)}) collective-permute-start(bf16[512,512]{1,0:T(8,128)(2,1)} %collective-permute-done.7.refs_3_), channel_id=1, source_target_pairs={{0,1},{1,0},{2,3},{3,2},{4,5},{5,4},{6,7},{7,6},{8,9},{9,8},{10,11... | collective-permute-start | bytes 1572872 | tf_op jit(solution)/shard_map/ppermute | solution.py:27
  60.9 0.7 copy-start.6
  61.6 4.2 %collective-permute-start.3 = (bf16[208,512]{1,0:T(8,128)(2,1)}, bf16[208,512]{1,0:T(8,128)(2,1)S(1)}, u32[]{:S(2)}, u32[]{:S(2)}) collective-permute-start(bf16[208,512]{1,0:T(8,128)(2,1)} %get-tuple-element.11), channel_id=1, source_target_pairs={{0,1},{1,0},{2,3},{3,2},{4,5},{5,4},{6,7},{7,6},{8,9},{9,8},{10,11... | collective-permute-start | bytes 638984 | tf_op jit(solution)/shard_map/ppermute | solution.py:27
  62.5 3.3 %collective-permute-start.4 = (bf16[16,2048]{1,0:T(8,128)(2,1)S(1)}, bf16[16,2048]{1,0:T(8,128)(2,1)S(1)}, u32[]{:S(2)}, u32[]{:S(2)}) collective-permute-start(bf16[16,2048]{1,0:T(8,128)(2,1)S(1)} %slice.32), channel_id=1, source_target_pairs={{0,1},{1,2},{2,3},{3,4},{4,5},{5,6},{6,7},{7,8},{8,9},{9,10},{10,1... | collective-permute-start | bytes 196616 | tf_op jit(solution)/shard_map/ppermute | solution.py:22
  65.8 1.1 %copy-start.5 = (bf16[192,2048]{1,0:T(8,128)(2,1)S(1)}, bf16[192,2048]{1,0:T(8,128)(2,1)}, u32[]{:S(2)}) copy-start(bf16[192,2048]{1,0:T(8,128)(2,1)} %stream.1) | copy-start | bytes 2359300
  66.9 0.9 copy-start.7
  67.9 12.3 %copy-start.9 = (bf16[2048,128]{1,0:T(8,128)(2,1)S(1)}, bf16[2048,128]{1,0:T(8,128)(2,1)}, u32[]{:S(2)}) copy-start(bf16[2048,128]{1,0:T(8,128)(2,1)} %param.18) | copy-start | bytes 1572868
  67.9 12.3 %copy-start.10 = (bf16[2048,128]{1,0:T(8,128)(2,1)S(1)}, bf16[2048,128]{1,0:T(8,128)(2,1)}, u32[]{:S(2)}) copy-start(bf16[2048,128]{1,0:T(8,128)(2,1)} %param.17) | copy-start | bytes 1572868
  67.9 12.3 %copy-start.11 = (bf16[2048,128]{1,0:T(8,128)(2,1)S(1)}, bf16[2048,128]{1,0:T(8,128)(2,1)}, u32[]{:S(2)}) copy-start(bf16[2048,128]{1,0:T(8,128)(2,1)} %param.16) | copy-start | bytes 1572868
  104.5 5.2 %collective-permute-start.12 = (bf16[24,2048]{1,0:T(8,128)(2,1)S(1)}, bf16[24,2048]{1,0:T(8,128)(2,1)S(1)}, u32[]{:S(2)}, u32[]{:S(2)}) collective-permute-start(bf16[24,2048]{1,0:T(8,128)(2,1)S(1)} %get-tuple-element.18), channel_id=1, source_target_pairs={{0,3},{1,2},{2,1},{3,0},{4,7},{5,6},{6,5},{7,4},{8,11},{9,10},{10,... | collective-permute-start | bytes 294920 | tf_op jit(solution)/shard_map/ppermute | solution.py:72
  104.5 6.0 %collective-permute-start.11 = (bf16[24,2048]{1,0:T(8,128)(2,1)S(1)}, bf16[24,2048]{1,0:T(8,128)(2,1)S(1)}, u32[]{:S(2)}, u32[]{:S(2)}) collective-permute-start(bf16[24,2048]{1,0:T(8,128)(2,1)S(1)} %get-tuple-element.19), channel_id=1, source_target_pairs={{0,2},{1,3},{2,0},{3,1},{4,6},{5,7},{6,4},{7,5},{8,10},{9,11},{10,... | collective-permute-start | bytes 294920 | tf_op jit(solution)/shard_map/ppermute | solution.py:72
  105.4 5.1 %collective-permute-start.10 = (bf16[24,2048]{1,0:T(8,128)(2,1)S(1)}, bf16[24,2048]{1,0:T(8,128)(2,1)S(1)}, u32[]{:S(2)}, u32[]{:S(2)}) collective-permute-start(bf16[24,2048]{1,0:T(8,128)(2,1)S(1)} %get-tuple-element.17), channel_id=1, source_target_pairs={{0,1},{1,0},{2,3},{3,2},{4,5},{5,4},{6,7},{7,6},{8,9},{9,8},{10,11... | collective-permute-start | bytes 294920 | tf_op jit(solution)/shard_map/ppermute | solution.py:72

commit v3 on v2

--- a/solution.py
+++ b/solution.py
@@ -50,7 +50,9 @@
         fetched.append((near, lax.ppermute(near, BOTH, mates)))
     pieces = [shard, swapped_cores(shard)]
     for near, far in fetched:
-        pieces += [near, far, swapped_cores(near), swapped_cores(far)]
+        near_mate = swapped_cores(near)
+        far_mate = swapped_cores(far)
+        pieces += [near, far, near_mate, far_mate]
     return pieces
 
 
@@ -75,7 +77,34 @@
     return own
 
 
-def attention_kernel(takes, query, key, value, mate, *refs):
+def pack_kernel(takes, query, key, value, q_mate, k_mate, v_mate, *refs):
+    blocks, (edges, sems) = refs[: len(takes)], refs[len(takes) :]
+    rows = query.shape[0]
+    width = edges.shape[2]
+    core = lax.axis_index("inner") % 2
+    own = pl.multiple_of(core * rows, 16)
+    other = pl.multiple_of((1 - core) * rows, 16)
+    columns = pl.ds(pl.multiple_of(core * width, 128), width)
+    last = pl.ds(rows - EXTRA, EXTRA)
+    moves = [
+        (query.at[last, columns], edges.at[0]),
+        (q_mate.at[last, columns], edges.at[1]),
+    ]
+    for ref, start, at in ((key, own, 0), (k_mate, other, 0), (value, own, 1), (v_mate, other, 1)):
+        moves.append((ref.at[:, columns], blocks[0].at[pl.ds(start, rows), pl.ds(at * width, width)]))
+    copies = [pltpu.make_async_copy(a, b, sems.at[i]) for i, (a, b) in enumerate(moves)]
+    for copy in copies:
+        copy.start()
+    for copy in copies:
+        copy.wait()
+    ahead = 2 * rows
+    blocks[0][ahead:, :width] = jnp.where(core == 1, edges[0], edges[1])
+    blocks[0][ahead:, width:] = jnp.zeros((EXTRA, width), jnp.bfloat16)
+    for take, block in zip(takes[1:], blocks[1:]):
+        block[...] = blocks[0][ahead - take : ahead, :]
+
+
+def attention_kernel(takes, query, key, value, q_mate, k_mate, v_mate, *refs):
     halos = refs[: len(takes)]
     mine_out, send_out, q_all, k_all, v_all, bias, sems = refs[len(takes) :]
     rows = query.shape[0]
@@ -96,9 +125,9 @@
     place(query.at[:, columns], q_all.at[pl.ds(EXTRA + own, rows)])
     place(key.at[:, columns], k_all.at[pl.ds(halo + own, rows)])
     place(value.at[:, columns], v_all.at[pl.ds(halo + own, rows)])
-    place(mate.at[:, pl.ds(0, width)], q_all.at[pl.ds(EXTRA + other, rows)])
-    place(mate.at[:, pl.ds(width, width)], k_all.at[pl.ds(halo + other, rows)])
-    place(mate.at[:, pl.ds(2 * width, width)], v_all.at[pl.ds(halo + other, rows)])
+    place(q_mate.at[:, columns], q_all.at[pl.ds(EXTRA + other, rows)])
+    place(k_mate.at[:, columns], k_all.at[pl.ds(halo + other, rows)])
+    place(v_mate.at[:, columns], v_all.at[pl.ds(halo + other, rows)])
     place(halos[0].at[pl.ds(takes[0], EXTRA), pl.ds(0, width)], q_all.at[pl.ds(0, EXTRA)])
     start = halo
     for take, ref in zip(takes, halos):
@@ -140,37 +169,43 @@
 def fine_attention(fine_query, fine_key, fine_value):
     rows, full = fine_query.shape
     width = full // 2
-    core = lax.axis_index("inner") % 2
-    away = (1 - core) * width
-    kept = core * width
     parts = (fine_query, fine_key, fine_value)
-    mate = swapped_cores(
-        jnp.concatenate([lax.dynamic_slice_in_dim(a, away, width, 1) for a in parts], axis=1)
-    )
-    mine = jnp.concatenate([lax.dynamic_slice_in_dim(a, kept, width, 1) for a in parts], axis=1)
-    low = jnp.where(core == 0, mine, mate)
-    high = jnp.where(core == 0, mate, mine)
+    mates = []
+    for part in parts:
+        mates.append(swapped_cores(part))
     left = -(-(WIN - 1 + EXTRA) // 16) * 16
     takes = []
     while left > 0:
         takes.append(min(left, 2 * rows))
         left -= takes[-1]
-    chip_kv = jnp.concatenate([low[:, width:], high[:, width:]], axis=0)
+    anywhere = pl.BlockSpec(memory_space=pl.ANY)
+    inside = pl.BlockSpec(memory_space=pltpu.VMEM)
+    heights = [2 * rows + EXTRA] + takes[1:]
+    blocks = pl.pallas_call(
+        functools.partial(pack_kernel, tuple(takes)),
+        out_shape=tuple(jax.ShapeDtypeStruct((h, full), jnp.bfloat16) for h in heights),
+        in_specs=[anywhere] * 6,
+        out_specs=(inside,) * len(takes),
+        scratch_shapes=[
+            pltpu.VMEM((2, EXTRA, width), jnp.bfloat16),
+            pltpu.SemaphoreType.DMA((6,)),
+        ],
+        compiler_params=pltpu.CompilerParams(vmem_limit_bytes=8 * 1024 * 1024),
+        cost_estimate=pl.CostEstimate(
+            flops=0, bytes_accessed=8 * rows * full, transcendentals=0
+        ),
+        name="pack",
+    )(*parts, *mates)
     halos = []
-    for at, take in enumerate(takes):
-        block = chip_kv[2 * rows - take :]
-        if at == 0:
-            edge = jnp.pad(high[rows - EXTRA :, :width], ((0, 0), (0, width)))
-            block = jnp.concatenate([block, edge], axis=0)
+    for at, block in enumerate(blocks):
         halos.append(on_ahead(block, 2 * (at + 1)))
     count, halo = rows + EXTRA, sum(takes)
-    anywhere = pl.BlockSpec(memory_space=pl.ANY)
     out = jax.ShapeDtypeStruct((count, width), jnp.bfloat16)
     pairs = 4 * (width // HE) * count * (halo + rows)
     return pl.pallas_call(
         functools.partial(attention_kernel, tuple(takes)),
         out_shape=(out, out),
-        in_specs=[anywhere] * (4 + len(takes)),
+        in_specs=[anywhere] * (6 + len(takes)),
         out_specs=(pl.BlockSpec(memory_space=pltpu.VMEM),) * 2,
         scratch_shapes=[
             pltpu.VMEM((2 * rows + EXTRA, width), jnp.bfloat16),
@@ -184,7 +219,7 @@
             flops=2 * pairs * HE, bytes_accessed=6 * rows * full, transcendentals=pairs // 2
         ),
         name="fine_attention",
-    )(fine_query, fine_key, fine_value, mate, *halos)
+    )(*parts, *mates, *halos)
 
 
 def state_kernel(counts, mix_mine, mix_mate, stream, edge, gain, *refs):
@@ -358,6 +393,7 @@
         P(None, "inner"),
         P("inner", None),
     )
+
     return jax.shard_map(
         on_device,
         mesh=mesh,

time: 112 us -> 110 us (0.982)
  other arithmetic: 3.59 us -> 1.35 us
  local copies, waits for them, and re-layouts: 7.25 us -> 8.9 us
    unnamed x24 -> x34, local copies, waits for them, and re-layouts: 2.78 us -> 6.85 us
    dynamic_slice x2 -> x0, local copies, waits for them, and re-layouts: 2.68 us -> none  [fine_attention(): lax.dynamic_slice_in_dim(a, kept, width, 1)]
    ppermute x5 -> x7, waiting for transfers between devices: 0.01 us -> 2.27 us  [swapped_cores(): return lax.ppermute(block, 'inner', [(i, i ^ 1) for i in range(count)])]
    concatenate x3 -> x0, other arithmetic: 2.17 us -> none  [the longest x1 1.26 us: fine_attention(): jnp.concatenate([lax.dynamic_slice_in_dim(a, kept, width, 1) for a in par...]
    ppermute x1, waiting for transfers between devices: 7.81 us -> 6.11 us  [shards_of_all(): lax.ppermute(part, 'inner', [(i, (i + hop) % count) for i in range(count)])]
    ppermute x3, starting transfers between devices: 7.77 us -> 6.49 us  [on_ahead(): lax.ppermute(block, BOTH, [(i, i + distance) for i in range(count - dista...]
  transfers between devices with their start and end apart: 13 -> 15, of which waited for: 6 -> 9; matrix products, arithmetic and copies ran while one was open for 3% -> 1% of each run, Pallas kernels for 4% -> 4%
where the time goes in v3:
time: 110 us
  blocking collectives  31.3 us (28%)
  starting transfers between devices  31.2 us (28%)
  waiting for transfers between devices  28.1 us (26%)
  local copies, waits for them, and re-layouts  8.9 us (8%)
  Pallas kernels  7.67 us (7%)
  other arithmetic  1.35 us (1%)
  matrix products  1.18 us (1%)
    ppermute x1, starting transfers between devices, shards_of_all(): fetched.append((near, lax.ppermute(near, BOTH, mates)))  19 us
    all_gather x1, blocking collectives, outer_gather(): lax.all_gather(near, 'outer', axis=0, tiled=True, axis_index_groups=lines)  16.5 us
    ppermute x1, waiting for transfers between devices, shards_of_all(): fetched.append((near, lax.ppermute(near, BOTH, mates)))  10.5 us
    all_gather x1, blocking collectives, on_device(): lax.all_gather(normed, 'inner', axis=0, tiled=True)  8.5 us
    unnamed x34, local copies, waits for them, and re-layouts  6.85 us
    ppermute x3, starting transfers between devices, on_ahead(): lax.ppermute(block, BOTH, [(i, i + distance) for i in range(count - dista...  6.49 us
    all_gather x1, blocking collectives, outer_gather(): lax.all_gather(block, 'outer', axis=0, tiled=True, axis_index_groups=pairs)  6.24 us
    ppermute x1, waiting for transfers between devices, shards_of_all(): lax.ppermute(part, 'inner', [(i, (i + hop) % count) for i in range(count)])  6.11 us
  transfers between devices with their start and end apart: 15, of which 9 were waited for; matrix products, arithmetic and copies ran while one was open for 1% of the time, Pallas kernels for 4%

profile of v3, /device:TPU:0, one launch (start us, length us, event | category | flops | bytes accessed | tf_op | source)
XLA Modules:
  0.0 109.9 jit_solution(18318045381566910076)
XLA Ops:
  0.0 1.2 %constant_dynamic-slice_fusion = bf16[512,512]{1,0:T(8,128)(2,1)S(1)} fusion(bf16[1024,512]{1,0:T(8,128)(2,1)} %refs_0_.1, s32[]{:T(128)S(6)} %select_n.52), kind=kLoop, calls=%fused_computation.34 | loop fusion | bytes 1048580 | tf_op jit(solution)/shard_map/dynamic_slice | solution.py:48
  1.2 3.1 %collective-permute-start.8 = (bf16[512,512]{1,0:T(8,128)(2,1)S(1)}, bf16[512,512]{1,0:T(8,128)(2,1)}, u32[]{:S(2)}, u32[]{:S(2)}) collective-permute-start(bf16[512,512]{1,0:T(8,128)(2,1)S(1)} %constant_dynamic-slice_fusion), channel_id=1, source_target_pairs={{0,2},{1,3},{2,0},{3,1},{4,6},{5,7},{6,4},{7,5},{8,10},{9,11},{10,... | collective-permute-start | bytes 1572872 | tf_op jit(solution)/shard_map/ppermute | solution.py:49
  4.9 1.1 %collective-permute-done.q_mate = bf16[192,1024]{1,0:T(8,128)(2,1)S(1)} collective-permute-done((bf16[192,1024]{1,0:T(8,128)(2,1)S(1)}, bf16[192,1024]{1,0:T(8,128)(2,1)S(1)}, u32[]{:S(2)}, u32[]{:S(2)}) %collective-permute-start) | collective-permute-done | bytes 393248 | tf_op jit(solution)/shard_map/ppermute | solution.py:27
  6.0 0.6 collective-permute-done.1.k_mate
  6.6 0.6 collective-permute-done.2.v_mate
  7.2 1.0 copy-done.4
  8.4 2.0 %collective-permute-start.3 = (bf16[400,1024]{1,0:T(8,128)(2,1)S(1)}, bf16[400,1024]{1,0:T(8,128)(2,1)S(1)}, u32[]{:S(2)}, u32[]{:S(2)}) collective-permute-start(bf16[400,1024]{1,0:T(8,128)(2,1)S(1)} %get-tuple-element.12), channel_id=1, source_target_pairs={{0,2},{1,3},{2,4},{3,5},{4,6},{5,7},{6,8},{7,9},{8,10},{9,11},{10,... | collective-permute-start | bytes 2457608 | tf_op jit(solution)/shard_map/ppermute | solution.py:22
  10.5 6.1 %collective-permute-done.8.refs_2_ = bf16[512,512]{1,0:T(8,128)(2,1)} collective-permute-done((bf16[512,512]{1,0:T(8,128)(2,1)S(1)}, bf16[512,512]{1,0:T(8,128)(2,1)}, u32[]{:S(2)}, u32[]{:S(2)}) %collective-permute-start.8) | collective-permute-done | bytes 524320 | tf_op jit(solution)/shard_map/ppermute | solution.py:49
  16.6 19.0 %collective-permute-start.9 = (bf16[512,512]{1,0:T(8,128)(2,1)}, bf16[512,512]{1,0:T(8,128)(2,1)}, u32[]{:S(2)}, u32[]{:S(2)}) collective-permute-start(bf16[512,512]{1,0:T(8,128)(2,1)} %collective-permute-done.8.refs_2_), channel_id=1, source_target_pairs={{0,4},{1,5},{2,10},{3,11},{4,0},{5,1},{6,14},{7,15},{8,12},{9,13},... | collective-permute-start | bytes 1572872 | tf_op jit(solution)/shard_map/ppermute | solution.py:50
  35.6 2.0 %collective-permute-start.4 = (bf16[144,1024]{1,0:T(8,128)(2,1)S(1)}, bf16[144,1024]{1,0:T(8,128)(2,1)S(1)}, u32[]{:S(2)}, u32[]{:S(2)}) collective-permute-start(bf16[144,1024]{1,0:T(8,128)(2,1)S(1)} %get-tuple-element.13), channel_id=1, source_target_pairs={{0,4},{1,5},{2,6},{3,7},{4,8},{5,9},{6,10},{7,11},{8,12},{9,13},{1... | collective-permute-start | bytes 884744 | tf_op jit(solution)/shard_map/ppermute | solution.py:22
  37.7 10.5 %collective-permute-done.9.refs_3_ = bf16[512,512]{1,0:T(8,128)(2,1)} collective-permute-done((bf16[512,512]{1,0:T(8,128)(2,1)}, bf16[512,512]{1,0:T(8,128)(2,1)}, u32[]{:S(2)}, u32[]{:S(2)}) %collective-permute-start.9) | collective-permute-done | bytes 524320 | tf_op jit(solution)/shard_map/ppermute | solution.py:50
  48.2 4.2 %collective-permute-done.4.refs_1_ = bf16[144,1024]{1,0:T(8,128)(2,1)S(1)} collective-permute-done((bf16[144,1024]{1,0:T(8,128)(2,1)S(1)}, bf16[144,1024]{1,0:T(8,128)(2,1)S(1)}, u32[]{:S(2)}, u32[]{:S(2)}) %collective-permute-start.4) | collective-permute-done | bytes 294944 | tf_op jit(solution)/shard_map/ppermute | solution.py:22
  52.5 4.1 %fine_attention.1 = (bf16[208,512]{1,0:T(8,128)(2,1)S(1)}, bf16[208,512]{1,0:T(8,128)(2,1)}) custom-call(bf16[192,1024]{1,0:T(8,128)(2,1)S(1)} %copy-done.2, bf16[192,1024]{1,0:T(8,128)(2,1)S(1)} %copy-done.3, bf16[192,1024]{1,0:T(8,128)(2,1)S(1)} %copy-done.5, bf16[192,1024]{1,0:T(8,128)(2,1)S(1)} %collective-permute-done.q_mate, ...), custom_call_target="tpu_custom_call" | custom-call | flops 613416960 | bytes 1179648 | tf_op jit(solution)/shard_map/fine_attention/pallas_call | solution.py:205
  56.6 0.7 copy-done.7
  57.3 0.8 slice.15
  58.2 2.4 %collective-permute-start.6 = (bf16[16,2048]{1,0:T(8,128)(2,1)S(1)}, bf16[16,2048]{1,0:T(8,128)(2,1)S(1)}, u32[]{:S(2)}, u32[]{:S(2)}) collective-permute-start(bf16[16,2048]{1,0:T(8,128)(2,1)S(1)} %slice.15), channel_id=1, source_target_pairs={{0,1},{1,2},{2,3},{3,4},{4,5},{5,6},{6,7},{7,8},{8,9},{9,10},{10,1... | collective-permute-start | bytes 196616 | tf_op jit(solution)/shard_map/ppermute | solution.py:22
  60.6 0.8 collective-permute-done.6.edge
  61.4 0.6 copy-done.11
  62.1 0.7 copy-done.9
  62.8 1.1 %copy-done.6 = bf16[192,2048]{1,0:T(8,128)(2,1)S(1)} copy-done((bf16[192,2048]{1,0:T(8,128)(2,1)S(1)}, bf16[192,2048]{1,0:T(8,128)(2,1)}, u32[]{:S(2)}) %copy-start.6) | copy-done | bytes 786456
  63.9 0.9 copy-done.8
  64.8 0.9 copy-done.10
  65.8 0.8 copy-done.12
  66.6 3.3 %fine_state.1 = (bf16[192,2048]{1,0:T(8,128)(2,1)S(1)}, bf16[24,2048]{1,0:T(8,128)(2,1)S(1)}, bf16[24,2048]{1,0:T(8,128)(2,1)S(1)}) custom-call(bf16[208,512]{1,0:T(8,128)(2,1)S(1)} %copy-done.8, bf16[208,512]{1,0:T(8,128)(2,1)S(1)} %copy-done.10, bf16[192,2048]{1,0:T(8,128)(2,1)S(1)} %copy-done.6, bf16[16,2048]{1,0:T(8,128)(2,1)S(1)} %copy-done.12, ...), custom_call_target="tpu_custom_call" | custom-call | flops 872415232 | bytes 5767168 | tf_op jit(solution)/shard_map/fine_state/pallas_call | solution.py:292
  70.0 8.5 %all_gather.9 = bf16[96,2048]{1,0:T(8,128)(2,1)S(1)} all-gather(bf16[24,2048]{1,0:T(8,128)(2,1)S(1)} %get-tuple-element.18), channel_id=1, replica_groups=mesh['outer'=8,'inner'=4] {'inner'}, dimensions={0}, use_global_device_ids=true | all-gather | bytes 491520 | tf_op jit(solution)/shard_map/all_gather | solution.py:341
  78.9 6.2 %all_gather.10 = bf16[192,256]{1,0:T(8,128)(2,1)S(1)} all-gather(bf16[96,256]{1,0:T(8,128)(2,1)S(1)} %slice.21), channel_id=1, replica_groups={{0,4},{8,12},{16,20},{24,28},{1,5},{9,13},{17,21},{25,29},{2,6},{10,14}..., dimensions={0}, use_global_device_ids=true | all-gather | bytes 147456 | tf_op jit(solution)/shard_map/all_gather | solution.py:63
  85.1 16.5 %all_gather.11 = bf16[768,256]{1,0:T(8,128)(2,1)S(1)} all-gather(bf16[192,256]{1,0:T(8,128)(2,1)S(1)} %all_gather.10), channel_id=1, replica_groups={{0,8,16,24},{4,12,20,28},{1,9,17,25},{5,13,21,29},{2,10,18,26},{6,14,22..., dimensions={0}, use_global_device_ids=true | all-gather | bytes 491520 | tf_op jit(solution)/shard_map/all_gather | solution.py:64
  102.8 0.9 collective-permute-start.13
  103.7 0.9 collective-permute-start.12
  104.6 3.2 %collective-permute-done.14 = bf16[24,2048]{1,0:T(8,128)(2,1)S(1)} collective-permute-done((bf16[24,2048]{1,0:T(8,128)(2,1)S(1)}, bf16[24,2048]{1,0:T(8,128)(2,1)S(1)}, u32[]{:S(2)}, u32[]{:S(2)}) %collective-permute-start.14) | collective-permute-done | bytes 98336 | tf_op jit(solution)/shard_map/ppermute | solution.py:74
  107.9 0.9 collective-permute-done.13
  108.9 1.1 fusion.6
  (49 shorter events, 2.6 us)
Async XLA Ops:
  0.0 102.2 %copy-start = (bf16[128,2048]{1,0:T(8,128)(2,1)S(1)}, bf16[128,2048]{1,0:T(8,128)(2,1)}, u32[]{:S(2)}) copy-start(bf16[128,2048]{1,0:T(8,128)(2,1)} %param.19) | copy-start | bytes 1572868
  0.0 4.3 %copy-start.2 = (bf16[192,1024]{1,0:T(8,128)(2,1)S(1)}, bf16[192,1024]{1,0:T(8,128)(2,1)}, u32[]{:S(2)}) copy-start(bf16[192,1024]{1,0:T(8,128)(2,1)} %query.3) | copy-start | bytes 1179652
  0.0 4.3 %copy-start.3 = (bf16[192,1024]{1,0:T(8,128)(2,1)S(1)}, bf16[192,1024]{1,0:T(8,128)(2,1)}, u32[]{:S(2)}) copy-start(bf16[192,1024]{1,0:T(8,128)(2,1)} %key.3) | copy-start | bytes 1179652
  1.2 9.2 %copy-start.1 = (bf16[1024,512]{1,0:T(8,128)(2,1)S(1)}, bf16[1024,512]{1,0:T(8,128)(2,1)}, u32[]{:S(2)}) copy-start(bf16[1024,512]{1,0:T(8,128)(2,1)} %refs_0_.1) | copy-start | bytes 3145732
  1.2 15.4 %collective-permute-start.8 = (bf16[512,512]{1,0:T(8,128)(2,1)S(1)}, bf16[512,512]{1,0:T(8,128)(2,1)}, u32[]{:S(2)}, u32[]{:S(2)}) collective-permute-start(bf16[512,512]{1,0:T(8,128)(2,1)S(1)} %constant_dynamic-slice_fusion), channel_id=1, source_target_pairs={{0,2},{1,3},{2,0},{3,1},{4,6},{5,7},{6,4},{7,5},{8,10},{9,11},{10,... | collective-permute-start | bytes 1572872 | tf_op jit(solution)/shard_map/ppermute | solution.py:49
  4.3 1.7 %collective-permute-start = (bf16[192,1024]{1,0:T(8,128)(2,1)S(1)}, bf16[192,1024]{1,0:T(8,128)(2,1)S(1)}, u32[]{:S(2)}, u32[]{:S(2)}) collective-permute-start(bf16[192,1024]{1,0:T(8,128)(2,1)S(1)} %copy-done.2), channel_id=1, source_target_pairs={{0,1},{1,0},{2,3},{3,2},{4,5},{5,4},{6,7},{7,6},{8,9},{9,8},{10,11... | collective-permute-start | bytes 1179656 | tf_op jit(solution)/shard_map/ppermute | solution.py:27
  4.3 2.3 %collective-permute-start.1 = (bf16[192,1024]{1,0:T(8,128)(2,1)S(1)}, bf16[192,1024]{1,0:T(8,128)(2,1)S(1)}, u32[]{:S(2)}, u32[]{:S(2)}) collective-permute-start(bf16[192,1024]{1,0:T(8,128)(2,1)S(1)} %copy-done.3), channel_id=1, source_target_pairs={{0,1},{1,0},{2,3},{3,2},{4,5},{5,4},{6,7},{7,6},{8,9},{9,8},{10,11... | collective-permute-start | bytes 1179656 | tf_op jit(solution)/shard_map/ppermute | solution.py:27
  4.8 2.3 %collective-permute-start.2 = (bf16[192,1024]{1,0:T(8,128)(2,1)}, bf16[192,1024]{1,0:T(8,128)(2,1)S(1)}, u32[]{:S(2)}, u32[]{:S(2)}) collective-permute-start(bf16[192,1024]{1,0:T(8,128)(2,1)} %value.3), channel_id=1, source_target_pairs={{0,1},{1,0},{2,3},{3,2},{4,5},{5,4},{6,7},{7,6},{8,9},{9,8},{10,11... | collective-permute-start | bytes 1179656 | tf_op jit(solution)/shard_map/ppermute | solution.py:27
  7.2 1.0 copy-start.4
  8.2 44.3 %copy-start.5 = (bf16[192,1024]{1,0:T(8,128)(2,1)S(1)}, bf16[192,1024]{1,0:T(8,128)(2,1)}, u32[]{:S(2)}) copy-start(bf16[192,1024]{1,0:T(8,128)(2,1)} %value.3) | copy-start | bytes 1179652
  8.4 44.1 %collective-permute-start.3 = (bf16[400,1024]{1,0:T(8,128)(2,1)S(1)}, bf16[400,1024]{1,0:T(8,128)(2,1)S(1)}, u32[]{:S(2)}, u32[]{:S(2)}) collective-permute-start(bf16[400,1024]{1,0:T(8,128)(2,1)S(1)} %get-tuple-element.12), channel_id=1, source_target_pairs={{0,2},{1,3},{2,4},{3,5},{4,6},{5,7},{6,8},{7,9},{8,10},{9,11},{10,... | collective-permute-start | bytes 2457608 | tf_op jit(solution)/shard_map/ppermute | solution.py:22
  10.4 51.6 %collective-permute-start.7 = (bf16[1024,512]{1,0:T(8,128)(2,1)S(1)}, bf16[1024,512]{1,0:T(8,128)(2,1)S(1)}, u32[]{:S(2)}, u32[]{:S(2)}) collective-permute-start(bf16[1024,512]{1,0:T(8,128)(2,1)S(1)} %copy-done.1), channel_id=1, source_target_pairs={{0,1},{1,0},{2,3},{3,2},{4,5},{5,4},{6,7},{7,6},{8,9},{9,8},{10,11... | collective-permute-start | bytes 3145736 | tf_op jit(solution)/shard_map/ppermute | solution.py:27
  16.6 31.6 %collective-permute-start.9 = (bf16[512,512]{1,0:T(8,128)(2,1)}, bf16[512,512]{1,0:T(8,128)(2,1)}, u32[]{:S(2)}, u32[]{:S(2)}) collective-permute-start(bf16[512,512]{1,0:T(8,128)(2,1)} %collective-permute-done.8.refs_2_), channel_id=1, source_target_pairs={{0,4},{1,5},{2,10},{3,11},{4,0},{5,1},{6,14},{7,15},{8,12},{9,13},... | collective-permute-start | bytes 1572872 | tf_op jit(solution)/shard_map/ppermute | solution.py:50
  35.6 27.2 %copy-start.13 = (f32[2048]{0:T(1024)S(1)}, f32[2048]{0:T(1024)}, u32[]{:S(2)}) copy-start(f32[2048]{0:T(1024)} %param.15) | copy-start | bytes 24580
  35.6 16.9 %collective-permute-start.4 = (bf16[144,1024]{1,0:T(8,128)(2,1)S(1)}, bf16[144,1024]{1,0:T(8,128)(2,1)S(1)}, u32[]{:S(2)}, u32[]{:S(2)}) collective-permute-start(bf16[144,1024]{1,0:T(8,128)(2,1)S(1)} %get-tuple-element.13), channel_id=1, source_target_pairs={{0,4},{1,5},{2,6},{3,7},{4,8},{5,9},{6,10},{7,11},{8,12},{9,13},{1... | collective-permute-start | bytes 884744 | tf_op jit(solution)/shard_map/ppermute | solution.py:22
  37.7 24.4 %collective-permute-start.10 = (bf16[512,512]{1,0:T(8,128)(2,1)}, bf16[512,512]{1,0:T(8,128)(2,1)}, u32[]{:S(2)}, u32[]{:S(2)}) collective-permute-start(bf16[512,512]{1,0:T(8,128)(2,1)} %collective-permute-done.8.refs_2_), channel_id=1, source_target_pairs={{0,1},{1,0},{2,3},{3,2},{4,5},{5,4},{6,7},{7,6},{8,9},{9,8},{10,11... | collective-permute-start | bytes 1572872 | tf_op jit(solution)/shard_map/ppermute | solution.py:27
  48.2 14.5 %collective-permute-start.11 = (bf16[512,512]{1,0:T(8,128)(2,1)}, bf16[512,512]{1,0:T(8,128)(2,1)}, u32[]{:S(2)}, u32[]{:S(2)}) collective-permute-start(bf16[512,512]{1,0:T(8,128)(2,1)} %collective-permute-done.9.refs_3_), channel_id=1, source_target_pairs={{0,1},{1,0},{2,3},{3,2},{4,5},{5,4},{6,7},{7,6},{8,9},{9,8},{10,11... | collective-permute-start | bytes 1572872 | tf_op jit(solution)/shard_map/ppermute | solution.py:27
  56.6 0.7 copy-start.7
  57.3 4.8 %collective-permute-start.5 = (bf16[208,512]{1,0:T(8,128)(2,1)}, bf16[208,512]{1,0:T(8,128)(2,1)S(1)}, u32[]{:S(2)}, u32[]{:S(2)}) collective-permute-start(bf16[208,512]{1,0:T(8,128)(2,1)} %get-tuple-element.15), channel_id=1, source_target_pairs={{0,1},{1,0},{2,3},{3,2},{4,5},{5,4},{6,7},{7,6},{8,9},{9,8},{10,11... | collective-permute-start | bytes 638984 | tf_op jit(solution)/shard_map/ppermute | solution.py:27
  58.2 3.3 %collective-permute-start.6 = (bf16[16,2048]{1,0:T(8,128)(2,1)S(1)}, bf16[16,2048]{1,0:T(8,128)(2,1)S(1)}, u32[]{:S(2)}, u32[]{:S(2)}) collective-permute-start(bf16[16,2048]{1,0:T(8,128)(2,1)S(1)} %slice.15), channel_id=1, source_target_pairs={{0,1},{1,2},{2,3},{3,4},{4,5},{5,6},{6,7},{7,8},{8,9},{9,10},{10,1... | collective-permute-start | bytes 196616 | tf_op jit(solution)/shard_map/ppermute | solution.py:22
  61.4 0.6 copy-start.11
  62.1 0.7 copy-start.9
  62.8 1.1 %copy-start.6 = (bf16[192,2048]{1,0:T(8,128)(2,1)S(1)}, bf16[192,2048]{1,0:T(8,128)(2,1)}, u32[]{:S(2)}) copy-start(bf16[192,2048]{1,0:T(8,128)(2,1)} %stream.1) | copy-start | bytes 2359300
  63.9 0.9 copy-start.8
  64.8 0.9 copy-start.10
  65.8 0.8 copy-start.12
  66.6 11.8 %copy-start.14 = (bf16[2048,128]{1,0:T(8,128)(2,1)S(1)}, bf16[2048,128]{1,0:T(8,128)(2,1)}, u32[]{:S(2)}) copy-start(bf16[2048,128]{1,0:T(8,128)(2,1)} %param.18) | copy-start | bytes 1572868
  66.6 11.8 %copy-start.15 = (bf16[2048,128]{1,0:T(8,128)(2,1)S(1)}, bf16[2048,128]{1,0:T(8,128)(2,1)}, u32[]{:S(2)}) copy-start(bf16[2048,128]{1,0:T(8,128)(2,1)} %param.17) | copy-start | bytes 1572868
  66.6 11.8 %copy-start.16 = (bf16[2048,128]{1,0:T(8,128)(2,1)S(1)}, bf16[2048,128]{1,0:T(8,128)(2,1)}, u32[]{:S(2)}) copy-start(bf16[2048,128]{1,0:T(8,128)(2,1)} %param.16) | copy-start | bytes 1572868
  102.7 5.2 %collective-permute-start.14 = (bf16[24,2048]{1,0:T(8,128)(2,1)S(1)}, bf16[24,2048]{1,0:T(8,128)(2,1)S(1)}, u32[]{:S(2)}, u32[]{:S(2)}) collective-permute-start(bf16[24,2048]{1,0:T(8,128)(2,1)S(1)} %get-tuple-element.20), channel_id=1, source_target_pairs={{0,3},{1,2},{2,1},{3,0},{4,7},{5,6},{6,5},{7,4},{8,11},{9,10},{10,... | collective-permute-start | bytes 294920 | tf_op jit(solution)/shard_map/ppermute | solution.py:74
  102.8 6.0 %collective-permute-start.13 = (bf16[24,2048]{1,0:T(8,128)(2,1)S(1)}, bf16[24,2048]{1,0:T(8,128)(2,1)S(1)}, u32[]{:S(2)}, u32[]{:S(2)}) collective-permute-start(bf16[24,2048]{1,0:T(8,128)(2,1)S(1)} %get-tuple-element.21), channel_id=1, source_target_pairs={{0,2},{1,3},{2,0},{3,1},{4,6},{5,7},{6,4},{7,5},{8,10},{9,11},{10,... | collective-permute-start | bytes 294920 | tf_op jit(solution)/shard_map/ppermute | solution.py:74
  103.7 5.1 %collective-permute-start.12 = (bf16[24,2048]{1,0:T(8,128)(2,1)S(1)}, bf16[24,2048]{1,0:T(8,128)(2,1)S(1)}, u32[]{:S(2)}, u32[]{:S(2)}) collective-permute-start(bf16[24,2048]{1,0:T(8,128)(2,1)S(1)} %get-tuple-element.19), channel_id=1, source_target_pairs={{0,1},{1,0},{2,3},{3,2},{4,5},{5,4},{6,7},{7,6},{8,9},{9,8},{10,11... | collective-permute-start | bytes 294920 | tf_op jit(solution)/shard_map/ppermute | solution.py:74

commit v4 on v3

--- a/solution.py
+++ b/solution.py
@@ -56,12 +56,76 @@
     return pieces
 
 
-def outer_gather(block):
+def outer_pieces(block):
     count = lax.axis_size("outer")
-    pairs = [[i, i + 1] for i in range(0, count, 2)]
-    lines = [list(range(i, count, 2)) for i in range(2)]
-    near = lax.all_gather(block, "outer", axis=0, tiled=True, axis_index_groups=pairs)
-    return lax.all_gather(near, "outer", axis=0, tiled=True, axis_index_groups=lines)
+    mate = lax.ppermute(block, "outer", [(i, i ^ 1) for i in range(count)])
+    both = jnp.concatenate([block, mate], axis=0)
+    return [both] + [
+        lax.ppermute(both, "outer", [(i, i ^ hop) for i in range(count)])
+        for hop in range(2, count, 2)
+    ]
+
+
+def coarse_kernel(length, projections, w_out, *refs):
+    pieces, out = refs[:-1], refs[-1]
+    width = w_out.shape[0]
+    outer = lax.axis_index("outer")
+    scale = 1.0 / math.sqrt(HE)
+    row = lax.broadcasted_iota(jnp.int32, (length, 2 * length), 0) + outer * length
+    col = lax.broadcasted_iota(jnp.int32, (length, 2 * length), 1)
+    second = col >= length
+    col = jnp.where(second, col - length, col)
+    mixes = []
+    for head in range(width // HE):
+        query = projections[:, head * HE : (head + 1) * HE]
+        top = total = summed = None
+        for at, piece in enumerate(pieces):
+            block = outer ^ (2 * at)
+            position = col + jnp.where(second, block ^ 1, block) * length
+            scores = lax.dot_general(
+                query,
+                piece[:, head * HE : (head + 1) * HE],
+                (((1,), (1,)), ((), ())),
+                preferred_element_type=jnp.float32,
+            )
+            scores = jnp.where(position <= row, scores * scale, very_negative)
+            high = jnp.max(scores, axis=-1, keepdims=True)
+            if at:
+                high = jnp.maximum(high, top)
+            weights = jnp.exp(scores - high)
+            part = jnp.sum(weights, axis=-1, keepdims=True)
+            mixed = jnp.dot(
+                weights.astype(jnp.bfloat16),
+                piece[:, width + head * HE : width + (head + 1) * HE],
+                preferred_element_type=jnp.float32,
+            )
+            if at:
+                shrink = jnp.exp(top - high)
+                part, mixed = part + total * shrink, mixed + summed * shrink
+            top, total, summed = high, part, mixed
+        mixes.append((summed / total).astype(jnp.bfloat16))
+    mix = mixes[0] if len(mixes) == 1 else jnp.concatenate(mixes, axis=1)
+    out[...] = jnp.dot(mix, w_out[...], preferred_element_type=jnp.float32).astype(jnp.bfloat16)
+
+
+def coarse_partial(projections, w_coarse_out, pieces):
+    length = projections.shape[0]
+    inside = pl.BlockSpec(memory_space=pltpu.VMEM)
+    keys = sum(piece.shape[0] for piece in pieces)
+    width, model_width = w_coarse_out.shape
+    return pl.pallas_call(
+        functools.partial(coarse_kernel, length),
+        out_shape=jax.ShapeDtypeStruct((length, model_width), jnp.bfloat16),
+        in_specs=[inside] * (2 + len(pieces)),
+        out_specs=inside,
+        compiler_params=pltpu.CompilerParams(vmem_limit_bytes=8 * 1024 * 1024 + 8 * keys * width),
+        cost_estimate=pl.CostEstimate(
+            flops=4 * length * keys * width + 2 * length * width * model_width,
+            bytes_accessed=4 * keys * width + 2 * (width + length) * model_width,
+            transcendentals=length * keys,
+        ),
+        name="coarse",
+    )(projections, w_coarse_out, *pieces)
 
 
 def summed_pieces(block):
@@ -77,8 +141,8 @@
     return own
 
 
-def pack_kernel(takes, query, key, value, q_mate, k_mate, v_mate, *refs):
-    blocks, (edges, sems) = refs[: len(takes)], refs[len(takes) :]
+def pack_kernel(takes, stream, query, key, value, q_mate, k_mate, v_mate, *refs):
+    blocks, (edge_out, edges, sems) = refs[: len(takes)], refs[len(takes) :]
     rows = query.shape[0]
     width = edges.shape[2]
     core = lax.axis_index("inner") % 2
@@ -89,6 +153,7 @@
     moves = [
         (query.at[last, columns], edges.at[0]),
         (q_mate.at[last, columns], edges.at[1]),
+        (stream.at[last], edge_out),
     ]
     for ref, start, at in ((key, own, 0), (k_mate, other, 0), (value, own, 1), (v_mate, other, 1)):
         moves.append((ref.at[:, columns], blocks[0].at[pl.ds(start, rows), pl.ds(at * width, width)]))
@@ -166,7 +231,7 @@
             out[:, lanes] = (summed / total).astype(jnp.bfloat16)
 
 
-def fine_attention(fine_query, fine_key, fine_value):
+def fine_attention(fine_input, fine_query, fine_key, fine_value):
     rows, full = fine_query.shape
     width = full // 2
     parts = (fine_query, fine_key, fine_value)
@@ -181,28 +246,30 @@
     anywhere = pl.BlockSpec(memory_space=pl.ANY)
     inside = pl.BlockSpec(memory_space=pltpu.VMEM)
     heights = [2 * rows + EXTRA] + takes[1:]
-    blocks = pl.pallas_call(
+    shapes = [(h, full) for h in heights] + [(EXTRA, fine_input.shape[1])]
+    *blocks, edge = pl.pallas_call(
         functools.partial(pack_kernel, tuple(takes)),
-        out_shape=tuple(jax.ShapeDtypeStruct((h, full), jnp.bfloat16) for h in heights),
-        in_specs=[anywhere] * 6,
-        out_specs=(inside,) * len(takes),
+        out_shape=tuple(jax.ShapeDtypeStruct(shape, jnp.bfloat16) for shape in shapes),
+        in_specs=[anywhere] * 7,
+        out_specs=(inside,) * len(shapes),
         scratch_shapes=[
             pltpu.VMEM((2, EXTRA, width), jnp.bfloat16),
-            pltpu.SemaphoreType.DMA((6,)),
+            pltpu.SemaphoreType.DMA((7,)),
         ],
-        compiler_params=pltpu.CompilerParams(vmem_limit_bytes=8 * 1024 * 1024),
+        compiler_params=pltpu.CompilerParams(vmem_limit_bytes=4 * 1024 * 1024),
         cost_estimate=pl.CostEstimate(
             flops=0, bytes_accessed=8 * rows * full, transcendentals=0
         ),
         name="pack",
-    )(*parts, *mates)
+    )(fine_input, *parts, *mates)
+    edge = on_ahead(edge, 1)
     halos = []
     for at, block in enumerate(blocks):
         halos.append(on_ahead(block, 2 * (at + 1)))
     count, halo = rows + EXTRA, sum(takes)
     out = jax.ShapeDtypeStruct((count, width), jnp.bfloat16)
     pairs = 4 * (width // HE) * count * (halo + rows)
-    return pl.pallas_call(
+    mixes = pl.pallas_call(
         functools.partial(attention_kernel, tuple(takes)),
         out_shape=(out, out),
         in_specs=[anywhere] * (6 + len(takes)),
@@ -214,17 +281,18 @@
             pltpu.VMEM((count, halo + rows), jnp.float32),
             pltpu.SemaphoreType.DMA((7 + 2 * len(takes),)),
         ],
-        compiler_params=pltpu.CompilerParams(vmem_limit_bytes=24 * 1024 * 1024),
+        compiler_params=pltpu.CompilerParams(vmem_limit_bytes=10 * 1024 * 1024),
         cost_estimate=pl.CostEstimate(
             flops=2 * pairs * HE, bytes_accessed=6 * rows * full, transcendentals=pairs // 2
         ),
         name="fine_attention",
     )(*parts, *mates, *halos)
+    return mixes, edge
 
 
 def state_kernel(counts, mix_mine, mix_mate, stream, edge, gain, *refs):
     pieces, refs = refs[: counts[0]], refs[counts[0] :]
-    state_out, pooled_out, normed_out, mix, weights, wide, sems = refs
+    state_out, pooled_out, normed_out, mix, weights, wide, rows_in, edge_in, sems = refs
     rows, model_width = stream.shape
     devices = lax.axis_size("inner")
     shard = model_width // devices
@@ -253,8 +321,21 @@
             group[-1].start()
         copies.append(group)
     width = depth // 2
-    mix[:, pl.ds(pl.multiple_of(core * width, 128), width)] = mix_mine[...]
-    mix[:, pl.ds(pl.multiple_of((1 - core) * width, 128), width)] = mix_mate[...]
+    kept = pl.ds(pl.multiple_of(core * width, 128), width)
+    given = pl.ds(pl.multiple_of((1 - core) * width, 128), width)
+    moves = (
+        (mix_mine, mix.at[:, kept]),
+        (mix_mate, mix.at[:, given]),
+        (edge, edge_in),
+        (stream, rows_in),
+    )
+    loads = [
+        pltpu.make_async_copy(a, b, sems.at[2 * devices + i]) for i, (a, b) in enumerate(moves)
+    ]
+    for load in loads:
+        load.start()
+    for load in loads:
+        load.wait()
     started = jnp.where(me + outer > 0, 1.0, 0.0)
     groups = rows // POOL
     moment = jnp.zeros((groups, 1), jnp.float32)
@@ -263,8 +344,8 @@
             copy.wait()
         columns = pl.ds(pl.multiple_of(owner * shard, 128), shard)
         projected = jnp.dot(mix[...], weights[slot], preferred_element_type=jnp.float32)
-        before = (edge[:, columns].astype(jnp.float32) + projected[:EXTRA]).astype(jnp.bfloat16)
-        state = (stream[:, columns].astype(jnp.float32) + projected[EXTRA:]).astype(jnp.bfloat16)
+        before = (edge_in[:, columns].astype(jnp.float32) + projected[:EXTRA]).astype(jnp.bfloat16)
+        state = (rows_in[:, columns].astype(jnp.float32) + projected[EXTRA:]).astype(jnp.bfloat16)
         state_out[:, columns] = state
         before = before[EXTRA - POOL :].astype(jnp.float32) * started
         cells = jnp.concatenate([before, state.astype(jnp.float32)], axis=0)
@@ -296,15 +377,17 @@
             jax.ShapeDtypeStruct((groups, model_width), jnp.bfloat16),
             jax.ShapeDtypeStruct((groups, model_width), jnp.bfloat16),
         ),
-        in_specs=[inside] * 5 + [anywhere] * len(pieces),
+        in_specs=[anywhere] * 4 + [inside] + [anywhere] * len(pieces),
         out_specs=(inside,) * 3,
         scratch_shapes=[
             pltpu.VMEM((rows + EXTRA, depth), jnp.bfloat16),
             pltpu.VMEM((devices, depth, shard), jnp.bfloat16),
             pltpu.VMEM((groups, model_width), jnp.float32),
-            pltpu.SemaphoreType.DMA((2 * devices,)),
+            pltpu.VMEM((rows, model_width), jnp.bfloat16),
+            pltpu.VMEM((EXTRA, model_width), jnp.bfloat16),
+            pltpu.SemaphoreType.DMA((2 * devices + 4,)),
         ],
-        compiler_params=pltpu.CompilerParams(vmem_limit_bytes=24 * 1024 * 1024),
+        compiler_params=pltpu.CompilerParams(vmem_limit_bytes=14 * 1024 * 1024),
         cost_estimate=pl.CostEstimate(
             flops=2 * (rows + EXTRA) * depth * model_width,
             bytes_accessed=2 * depth * model_width + 4 * rows * model_width,
@@ -327,10 +410,8 @@
     w_coarse_out,
 ):
     tok_rows, model_width = fine_input.shape
-    score_scale = 1.0 / math.sqrt(HE)
-    edge = on_ahead(fine_input[tok_rows - EXTRA :], 1)
     pieces = shards_of_all(w_fine_out)
-    mix_mine, mix_send = fine_attention(fine_query, fine_key, fine_value)
+    (mix_mine, mix_send), edge = fine_attention(fine_input, fine_query, fine_key, fine_value)
     mixes = (mix_mine, swapped_cores(mix_send))
     fine_state, pooled, normed = fine_state_of(mixes, fine_input, edge, norm_gain, pieces)
     pooled_wide = pooled.astype(jnp.float32)
@@ -342,38 +423,10 @@
         joined_weights,
         preferred_element_type=jnp.float32,
     ).astype(jnp.bfloat16)
-    group_len = projections.shape[0]
-    coarse_query = projections[:, :head_width].reshape(group_len, local_heads, HE)
-    outer_index = lax.axis_index("outer")
-    query_pos = outer_index * group_len + jnp.arange(group_len, dtype=jnp.int32)
-    gathered = outer_gather(projections[:, head_width:])
-    count = gathered.shape[0]
-    block_keys = gathered[:, :head_width].reshape(count, local_heads, HE)
-    block_values = gathered[:, head_width:].reshape(count, local_heads, HE)
-    block_scores = (
-        jnp.einsum("qhe,khe->hqk", coarse_query, block_keys, preferred_element_type=jnp.float32)
-        * score_scale
+    partial = coarse_partial(
+        projections[:, :head_width], w_coarse_out, outer_pieces(projections[:, head_width:])
     )
-    key_pos = jnp.arange(count, dtype=jnp.int32)
-    visible = (key_pos[None, :] <= query_pos[:, None])[None]
-    block_masked = jnp.where(visible, block_scores, very_negative)
-    new_max = jnp.max(block_masked, axis=-1)
-    block_exp = jnp.where(visible, jnp.exp(block_scores - new_max[:, :, None]), 0.0)
-    new_sum = jnp.sum(block_exp, axis=-1)
-    contrib = jnp.einsum(
-        "hqk,khe->hqe",
-        block_exp.astype(jnp.bfloat16),
-        block_values,
-        preferred_element_type=jnp.float32,
-    )
-    coarse_mix = (
-        jnp.transpose(contrib / new_sum[:, :, None], (1, 0, 2))
-        .reshape(group_len, head_width)
-        .astype(jnp.bfloat16)
-    )
-    head_total = summed_pieces(
-        jnp.dot(coarse_mix, w_coarse_out, preferred_element_type=jnp.float32).astype(jnp.bfloat16)
-    )
+    head_total = summed_pieces(partial)
     coarse_out = (pooled_wide + head_total).astype(jnp.bfloat16)
     fine_groups = fine_state.reshape(tok_rows // POOL, POOL, model_width).astype(jnp.float32)
     lifted = fine_groups + coarse_out.astype(jnp.float32)[:, None, :]

time: 110 us -> 96.6 us (0.88)
  blocking collectives: 31.3 us -> 8.5 us
  starting transfers between devices: 31.2 us -> 43.6 us
  local copies, waits for them, and re-layouts: 8.9 us -> 4.22 us
  Pallas kernels: 7.67 us -> 9.02 us
    all_gather x2 -> x0, blocking collectives: 22.8 us -> none  [the longest x1 16.5 us: outer_gather(): lax.all_gather(near, 'outer', axis=0, tiled=True, axis_index_groups=lines)]
    ppermute x0 -> x4, starting transfers between devices: none -> 13.2 us  [the longest x1 6.81 us: outer_pieces(): mate = lax.ppermute(block, 'outer', [(i, i ^ 1) for i in range(count)])]
    ppermute x0 -> x4, waiting for transfers between devices: none -> 9.47 us  [the longest x3 7.21 us: outer_pieces(): lax.ppermute(both, 'outer', [(i, i ^ hop) for i in range(count)])]
    ppermute x1, waiting for transfers between devices: 10.5 us -> 5.02 us  [shards_of_all(): fetched.append((near, lax.ppermute(near, BOTH, mates)))]
    unnamed x34 -> x26, local copies, waits for them, and re-layouts: 6.85 us -> 3.03 us
    ppermute x1, waiting for transfers between devices: 6.11 us -> 3.67 us  [shards_of_all(): lax.ppermute(part, 'inner', [(i, (i + hop) % count) for i in range(count)])]
    ppermute x3, waiting for transfers between devices: 5.08 us -> 3.58 us  [on_ahead(): lax.ppermute(block, BOTH, [(i, i + distance) for i in range(count - dista...]
    pallas_call x0 -> x1, Pallas kernels: none -> 1.38 us  [coarse_partial(): pl.pallas_call(functools.partial(coarse_kernel, length), out_shape=jax.Sh...]
  transfers between devices with their start and end apart: 15 -> 19, of which waited for: 9 -> 12; matrix products, arithmetic and copies ran while one was open for 1% -> 0% of each run, Pallas kernels for 4% -> 4%
where the time goes in v4:
time: 96.6 us; the launch traced here: 96.2 us
  starting transfers between devices  43.6 us (45%)
  waiting for transfers between devices  29.1 us (30%)
  Pallas kernels  9.02 us (9%)
  blocking collectives  8.5 us (9%)
  local copies, waits for them, and re-layouts  4.22 us (4%)
  other arithmetic  1.12 us (1%)
    ppermute x1, starting transfers between devices, shards_of_all(): fetched.append((near, lax.ppermute(near, BOTH, mates)))  18.1 us
    all_gather x1, blocking collectives, on_device(): lax.all_gather(normed, 'inner', axis=0, tiled=True)  8.5 us
    ppermute x3, waiting for transfers between devices, outer_pieces(): lax.ppermute(both, 'outer', [(i, i ^ hop) for i in range(count)])  7.21 us
    ppermute x1, starting transfers between devices, outer_pieces(): mate = lax.ppermute(block, 'outer', [(i, i ^ 1) for i in range(count)])  6.81 us
    ppermute x3, starting transfers between devices, on_ahead(): lax.ppermute(block, BOTH, [(i, i + distance) for i in range(count - dista...  6.6 us
    ppermute x3, starting transfers between devices, outer_pieces(): lax.ppermute(both, 'outer', [(i, i ^ hop) for i in range(count)])  6.4 us
    ppermute x1, waiting for transfers between devices, shards_of_all(): fetched.append((near, lax.ppermute(near, BOTH, mates)))  5.02 us
    ppermute x3, waiting for transfers between devices, summed_pieces(): lax.ppermute(piece, 'inner', [(i, i ^ hop) for i in range(count)])  4.8 us
  transfers between devices with their start and end apart: 19, of which 12 were waited for; matrix products, arithmetic and copies ran while one was open for 0% of the time, Pallas kernels for 4%

profile of v4, /device:TPU:0, one launch (start us, length us, event | category | flops | bytes accessed | tf_op | source)
XLA Modules:
  0.0 96.2 jit_solution(6076769909309261976)
XLA Ops:
  0.0 1.1 %constant_dynamic-slice_fusion = bf16[512,512]{1,0:T(8,128)(2,1)S(1)} fusion(bf16[1024,512]{1,0:T(8,128)(2,1)} %refs_0_.1, s32[]{:T(128)S(6)} %select_n.43), kind=kLoop, calls=%fused_computation.19 | loop fusion | bytes 1048580 | tf_op jit(solution)/shard_map/dynamic_slice | solution.py:48
  1.2 3.1 %collective-permute-start.8 = (bf16[512,512]{1,0:T(8,128)(2,1)S(1)}, bf16[512,512]{1,0:T(8,128)(2,1)S(1)}, u32[]{:S(2)}, u32[]{:S(2)}) collective-permute-start(bf16[512,512]{1,0:T(8,128)(2,1)S(1)} %constant_dynamic-slice_fusion), channel_id=1, source_target_pairs={{0,2},{1,3},{2,0},{3,1},{4,6},{5,7},{6,4},{7,5},{8,10},{9,11},{10,... | collective-permute-start | bytes 1572872 | tf_op jit(solution)/shard_map/ppermute | solution.py:49
  4.2 0.5 collective-permute-start.1
  4.7 1.4 %collective-permute-done.q_mate = bf16[192,1024]{1,0:T(8,128)(2,1)S(1)} collective-permute-done((bf16[192,1024]{1,0:T(8,128)(2,1)}, bf16[192,1024]{1,0:T(8,128)(2,1)S(1)}, u32[]{:S(2)}, u32[]{:S(2)}) %collective-permute-start) | collective-permute-done | bytes 393248 | tf_op jit(solution)/shard_map/ppermute | solution.py:27
  6.2 0.6 collective-permute-done.1.k_mate
  6.7 0.6 collective-permute-done.2.v_mate
  7.3 1.0 %copy-done.2 = bf16[192,1024]{1,0:T(8,128)(2,1)S(1)} copy-done((bf16[192,1024]{1,0:T(8,128)(2,1)S(1)}, bf16[192,1024]{1,0:T(8,128)(2,1)}, u32[]{:S(2)}) %copy-start.2) | copy-done | bytes 393240
  8.3 1.0 %copy-done.4 = bf16[192,1024]{1,0:T(8,128)(2,1)S(1)} copy-done((bf16[192,1024]{1,0:T(8,128)(2,1)S(1)}, bf16[192,1024]{1,0:T(8,128)(2,1)}, u32[]{:S(2)}) %copy-start.4) | copy-done | bytes 393240
  9.3 1.0 %copy-done.6 = bf16[192,1024]{1,0:T(8,128)(2,1)S(1)} copy-done((bf16[192,1024]{1,0:T(8,128)(2,1)S(1)}, bf16[192,1024]{1,0:T(8,128)(2,1)}, u32[]{:S(2)}) %copy-start.6) | copy-done | bytes 393240
  10.6 2.2 %collective-permute-start.3 = (bf16[400,1024]{1,0:T(8,128)(2,1)S(1)}, bf16[400,1024]{1,0:T(8,128)(2,1)S(1)}, u32[]{:S(2)}, u32[]{:S(2)}) collective-permute-start(bf16[400,1024]{1,0:T(8,128)(2,1)S(1)} %get-tuple-element.13), channel_id=1, source_target_pairs={{0,2},{1,3},{2,4},{3,5},{4,6},{5,7},{6,8},{7,9},{8,10},{9,11},{10,... | collective-permute-start | bytes 2457608 | tf_op jit(solution)/shard_map/ppermute | solution.py:22
  12.9 3.7 %collective-permute-done.8.refs_2_ = bf16[512,512]{1,0:T(8,128)(2,1)S(1)} collective-permute-done((bf16[512,512]{1,0:T(8,128)(2,1)S(1)}, bf16[512,512]{1,0:T(8,128)(2,1)S(1)}, u32[]{:S(2)}, u32[]{:S(2)}) %collective-permute-start.8) | collective-permute-done | bytes 524320 | tf_op jit(solution)/shard_map/ppermute | solution.py:49
  16.5 18.1 %collective-permute-start.9 = (bf16[512,512]{1,0:T(8,128)(2,1)S(1)}, bf16[512,512]{1,0:T(8,128)(2,1)S(1)}, u32[]{:S(2)}, u32[]{:S(2)}) collective-permute-start(bf16[512,512]{1,0:T(8,128)(2,1)S(1)} %collective-permute-done.8.refs_2_), channel_id=1, source_target_pairs={{0,4},{1,5},{2,10},{3,11},{4,0},{5,1},{6,14},{7,15},{8,12},{9,13},... | collective-permute-start | bytes 1572872 | tf_op jit(solution)/shard_map/ppermute | solution.py:50
  34.7 2.0 %collective-permute-start.4 = (bf16[144,1024]{1,0:T(8,128)(2,1)S(1)}, bf16[144,1024]{1,0:T(8,128)(2,1)S(1)}, u32[]{:S(2)}, u32[]{:S(2)}) collective-permute-start(bf16[144,1024]{1,0:T(8,128)(2,1)S(1)} %get-tuple-element.14), channel_id=1, source_target_pairs={{0,4},{1,5},{2,6},{3,7},{4,8},{5,9},{6,10},{7,11},{8,12},{9,13},{1... | collective-permute-start | bytes 884744 | tf_op jit(solution)/shard_map/ppermute | solution.py:22
  36.8 5.0 %collective-permute-done.9.refs_3_ = bf16[512,512]{1,0:T(8,128)(2,1)S(1)} collective-permute-done((bf16[512,512]{1,0:T(8,128)(2,1)S(1)}, bf16[512,512]{1,0:T(8,128)(2,1)S(1)}, u32[]{:S(2)}, u32[]{:S(2)}) %collective-permute-start.9) | collective-permute-done | bytes 524320 | tf_op jit(solution)/shard_map/ppermute | solution.py:50
  41.8 2.7 %collective-permute-done.4.refs_1_ = bf16[144,1024]{1,0:T(8,128)(2,1)S(1)} collective-permute-done((bf16[144,1024]{1,0:T(8,128)(2,1)S(1)}, bf16[144,1024]{1,0:T(8,128)(2,1)S(1)}, u32[]{:S(2)}, u32[]{:S(2)}) %collective-permute-start.4) | collective-permute-done | bytes 294944 | tf_op jit(solution)/shard_map/ppermute | solution.py:22
  44.5 3.6 %fine_attention.1 = (bf16[208,512]{1,0:T(8,128)(2,1)S(1)}, bf16[208,512]{1,0:T(8,128)(2,1)S(1)}) custom-call(bf16[192,1024]{1,0:T(8,128)(2,1)S(1)} %copy-done.3, bf16[192,1024]{1,0:T(8,128)(2,1)S(1)} %copy-done.5, bf16[192,1024]{1,0:T(8,128)(2,1)S(1)} %copy-done.7, bf16[192,1024]{1,0:T(8,128)(2,1)S(1)} %collective-permute-done.q_mate, ...), custom_call_target="tpu_custom_call" | custom-call | flops 613416960 | bytes 1179648 | tf_op jit(solution)/shard_map/fine_attention/pallas_call | solution.py:272
  48.2 2.4 %collective-permute-start.6 = (bf16[16,2048]{1,0:T(8,128)(2,1)S(1)}, bf16[16,2048]{1,0:T(8,128)(2,1)S(1)}, u32[]{:S(2)}, u32[]{:S(2)}) collective-permute-start(bf16[16,2048]{1,0:T(8,128)(2,1)S(1)} %get-tuple-element.17), channel_id=1, source_target_pairs={{0,1},{1,2},{2,3},{3,4},{4,5},{5,6},{6,7},{7,8},{8,9},{9,10},{10,1... | collective-permute-start | bytes 196616 | tf_op jit(solution)/shard_map/ppermute | solution.py:22
  50.6 0.9 collective-permute-done.6.edge
  51.6 3.7 %fine_state.1 = (bf16[192,2048]{1,0:T(8,128)(2,1)S(1)}, bf16[24,2048]{1,0:T(8,128)(2,1)S(1)}, bf16[24,2048]{1,0:T(8,128)(2,1)S(1)}) custom-call(bf16[208,512]{1,0:T(8,128)(2,1)S(1)} %get-tuple-element.15.mix_mine, bf16[208,512]{1,0:T(8,128)(2,1)S(1)} %collective-permute-done.5.mix_mate, bf16[192,2048]{1,0:T(8,128)(2,1)S(1)} %copy-done, ...), custom_call_target="tpu_custom_call" | custom-call | flops 872415232 | bytes 5767168 | tf_op jit(solution)/shard_map/fine_state/pallas_call | solution.py:373
  55.3 8.5 %all_gather.3 = bf16[96,2048]{1,0:T(8,128)(2,1)S(1)} all-gather(bf16[24,2048]{1,0:T(8,128)(2,1)S(1)} %get-tuple-element.20), channel_id=1, replica_groups=mesh['outer'=8,'inner'=4] {'inner'}, dimensions={0}, use_global_device_ids=true | all-gather | bytes 491520 | tf_op jit(solution)/shard_map/all_gather | solution.py:422
  64.2 6.8 %collective-permute-start.12 = (bf16[96,256]{1,0:T(8,128)(2,1)S(1)}, bf16[96,256]{1,0:T(8,128)(2,1)S(1)}, u32[]{:S(2)}, u32[]{:S(2)}) collective-permute-start(bf16[96,256]{1,0:T(8,128)(2,1)S(1)} %slice.9), channel_id=1, source_target_pairs={{0,4},{4,0},{8,12},{12,8},{16,20},{20,16},{24,28},{28,24},{1,5},{5... | collective-permute-start | bytes 147464 | tf_op jit(solution)/shard_map/ppermute | solution.py:61
  71.0 2.3 %collective-permute-done.12 = bf16[96,256]{1,0:T(8,128)(2,1)S(1)} collective-permute-done((bf16[96,256]{1,0:T(8,128)(2,1)S(1)}, bf16[96,256]{1,0:T(8,128)(2,1)S(1)}, u32[]{:S(2)}, u32[]{:S(2)}) %collective-permute-start.12) | collective-permute-done | bytes 49184 | tf_op jit(solution)/shard_map/ppermute | solution.py:61
  73.3 3.8 %collective-permute-start.13 = (bf16[192,256]{1,0:T(8,128)(2,1)S(1)}, bf16[192,256]{1,0:T(8,128)(2,1)S(1)}, u32[]{:S(2)}, u32[]{:S(2)}) collective-permute-start(bf16[192,256]{1,0:T(8,128)(2,1)S(1)} %pad_maximum_fusion.refs_0_), channel_id=1, source_target_pairs={{0,8},{4,12},{8,0},{12,4},{16,24},{20,28},{24,16},{28,20},{1,9},{5... | collective-permute-start | bytes 294920 | tf_op jit(solution)/shard_map/ppermute | solution.py:64
  77.1 2.6 %collective-permute-start.14 = (bf16[192,256]{1,0:T(8,128)(2,1)S(1)}, bf16[192,256]{1,0:T(8,128)(2,1)S(1)}, u32[]{:S(2)}, u32[]{:S(2)}) collective-permute-start(bf16[192,256]{1,0:T(8,128)(2,1)S(1)} %pad_maximum_fusion.refs_0_), channel_id=1, source_target_pairs={{0,16},{4,20},{8,24},{12,28},{16,0},{20,4},{24,8},{28,12},{1,17},{... | collective-permute-start | bytes 294920 | tf_op jit(solution)/shard_map/ppermute | solution.py:64
  79.7 0.8 collective-permute-done.13.refs_1_
  80.5 6.4 %collective-permute-done.14.refs_2_ = bf16[192,256]{1,0:T(8,128)(2,1)S(1)} collective-permute-done((bf16[192,256]{1,0:T(8,128)(2,1)S(1)}, bf16[192,256]{1,0:T(8,128)(2,1)S(1)}, u32[]{:S(2)}, u32[]{:S(2)}) %collective-permute-start.14) | collective-permute-done | bytes 98336 | tf_op jit(solution)/shard_map/ppermute | solution.py:64
  86.9 1.4 %coarse.1 = bf16[96,2048]{1,0:T(8,128)(2,1)S(1)} custom-call(bf16[96,128]{1,0:T(8,128)(2,1)S(1)} %slice.8.projections, bf16[128,2048]{1,0:T(8,128)(2,1)S(1)} %copy-done.8, bf16[192,256]{1,0:T(8,128)(2,1)S(1)} %pad_maximum_fusion.refs_0_, bf16[192,256]{1,0:T(8,128)(2,1)S(1)} %collective-permute-done.13.refs_1_, ...), custom_call_target="tpu_custom_call" | custom-call | flops 88080384 | bytes 1310720 | tf_op jit(solution)/shard_map/coarse/pallas_call | solution.py:116
  88.4 1.2 %collective-permute-start.17 = (bf16[24,2048]{1,0:T(8,128)(2,1)S(1)}, bf16[24,2048]{1,0:T(8,128)(2,1)S(1)}, u32[]{:S(2)}, u32[]{:S(2)}) collective-permute-start(bf16[24,2048]{1,0:T(8,128)(2,1)S(1)} %get-tuple-element.23), channel_id=1, source_target_pairs={{0,2},{1,3},{2,0},{3,1},{4,6},{5,7},{6,4},{7,5},{8,10},{9,11},{10,... | collective-permute-start | bytes 294920 | tf_op jit(solution)/shard_map/ppermute | solution.py:138
  89.7 0.6 collective-permute-start.16
  90.3 3.2 %collective-permute-done.18 = bf16[24,2048]{1,0:T(8,128)(2,1)S(1)} collective-permute-done((bf16[24,2048]{1,0:T(8,128)(2,1)S(1)}, bf16[24,2048]{1,0:T(8,128)(2,1)S(1)}, u32[]{:S(2)}, u32[]{:S(2)}) %collective-permute-start.18) | collective-permute-done | bytes 98336 | tf_op jit(solution)/shard_map/ppermute | solution.py:138
  93.5 1.6 %collective-permute-done.17 = bf16[24,2048]{1,0:T(8,128)(2,1)S(1)} collective-permute-done((bf16[24,2048]{1,0:T(8,128)(2,1)S(1)}, bf16[24,2048]{1,0:T(8,128)(2,1)S(1)}, u32[]{:S(2)}, u32[]{:S(2)}) %collective-permute-start.17) | collective-permute-done | bytes 98336 | tf_op jit(solution)/shard_map/ppermute | solution.py:138
  95.2 1.1 %fusion.6 = bf16[192,2048]{1,0:T(8,128)(2,1)} fusion(bf16[192,2048]{1,0:T(8,128)(2,1)S(1)} %get-tuple-element.18, f32[24,2048]{1,0:T(8,128)S(1)} %fusion.14), kind=kLoop, calls=%fused_computation.7 | loop fusion | flops 1179648 | bytes 1769472 | tf_op jit(solution)/shard_map/convert_element_type | solution.py:433
  (45 shorter events, 1.2 us)
Async XLA Ops:
  0.0 7.3 %copy-start = (bf16[192,2048]{1,0:T(8,128)(2,1)S(1)}, bf16[192,2048]{1,0:T(8,128)(2,1)}, u32[]{:S(2)}) copy-start(bf16[192,2048]{1,0:T(8,128)(2,1)} %stream.3) | copy-start | bytes 2359300
  1.2 11.6 %copy-start.1 = (bf16[1024,512]{1,0:T(8,128)(2,1)S(1)}, bf16[1024,512]{1,0:T(8,128)(2,1)}, u32[]{:S(2)}) copy-start(bf16[1024,512]{1,0:T(8,128)(2,1)} %refs_0_.1) | copy-start | bytes 3145732
  1.2 15.4 %collective-permute-start.8 = (bf16[512,512]{1,0:T(8,128)(2,1)S(1)}, bf16[512,512]{1,0:T(8,128)(2,1)S(1)}, u32[]{:S(2)}, u32[]{:S(2)}) collective-permute-start(bf16[512,512]{1,0:T(8,128)(2,1)S(1)} %constant_dynamic-slice_fusion), channel_id=1, source_target_pairs={{0,2},{1,3},{2,0},{3,1},{4,6},{5,7},{6,4},{7,5},{8,10},{9,11},{10,... | collective-permute-start | bytes 1572872 | tf_op jit(solution)/shard_map/ppermute | solution.py:49
  4.2 1.9 %collective-permute-start = (bf16[192,1024]{1,0:T(8,128)(2,1)}, bf16[192,1024]{1,0:T(8,128)(2,1)S(1)}, u32[]{:S(2)}, u32[]{:S(2)}) collective-permute-start(bf16[192,1024]{1,0:T(8,128)(2,1)} %query.3), channel_id=1, source_target_pairs={{0,1},{1,0},{2,3},{3,2},{4,5},{5,4},{6,7},{7,6},{8,9},{9,8},{10,11... | collective-permute-start | bytes 1179656 | tf_op jit(solution)/shard_map/ppermute | solution.py:27
  4.2 2.5 %collective-permute-start.1 = (bf16[192,1024]{1,0:T(8,128)(2,1)}, bf16[192,1024]{1,0:T(8,128)(2,1)S(1)}, u32[]{:S(2)}, u32[]{:S(2)}) collective-permute-start(bf16[192,1024]{1,0:T(8,128)(2,1)} %key.3), channel_id=1, source_target_pairs={{0,1},{1,0},{2,3},{3,2},{4,5},{5,4},{6,7},{7,6},{8,9},{9,8},{10,11... | collective-permute-start | bytes 1179656 | tf_op jit(solution)/shard_map/ppermute | solution.py:27
  4.7 2.5 %collective-permute-start.2 = (bf16[192,1024]{1,0:T(8,128)(2,1)}, bf16[192,1024]{1,0:T(8,128)(2,1)S(1)}, u32[]{:S(2)}, u32[]{:S(2)}) collective-permute-start(bf16[192,1024]{1,0:T(8,128)(2,1)} %value.3), channel_id=1, source_target_pairs={{0,1},{1,0},{2,3},{3,2},{4,5},{5,4},{6,7},{7,6},{8,9},{9,8},{10,11... | collective-permute-start | bytes 1179656 | tf_op jit(solution)/shard_map/ppermute | solution.py:27
  7.3 1.0 %copy-start.2 = (bf16[192,1024]{1,0:T(8,128)(2,1)S(1)}, bf16[192,1024]{1,0:T(8,128)(2,1)}, u32[]{:S(2)}) copy-start(bf16[192,1024]{1,0:T(8,128)(2,1)} %query.3) | copy-start | bytes 1179652
  8.3 1.0 %copy-start.4 = (bf16[192,1024]{1,0:T(8,128)(2,1)S(1)}, bf16[192,1024]{1,0:T(8,128)(2,1)}, u32[]{:S(2)}) copy-start(bf16[192,1024]{1,0:T(8,128)(2,1)} %key.3) | copy-start | bytes 1179652
  9.3 1.0 %copy-start.6 = (bf16[192,1024]{1,0:T(8,128)(2,1)S(1)}, bf16[192,1024]{1,0:T(8,128)(2,1)}, u32[]{:S(2)}) copy-start(bf16[192,1024]{1,0:T(8,128)(2,1)} %value.3) | copy-start | bytes 1179652
  10.3 34.2 %copy-start.3 = (bf16[192,1024]{1,0:T(8,128)(2,1)S(1)}, bf16[192,1024]{1,0:T(8,128)(2,1)}, u32[]{:S(2)}) copy-start(bf16[192,1024]{1,0:T(8,128)(2,1)} %query.3) | copy-start | bytes 1179652
  10.3 34.2 %copy-start.5 = (bf16[192,1024]{1,0:T(8,128)(2,1)S(1)}, bf16[192,1024]{1,0:T(8,128)(2,1)}, u32[]{:S(2)}) copy-start(bf16[192,1024]{1,0:T(8,128)(2,1)} %key.3) | copy-start | bytes 1179652
  10.3 34.2 %copy-start.7 = (bf16[192,1024]{1,0:T(8,128)(2,1)S(1)}, bf16[192,1024]{1,0:T(8,128)(2,1)}, u32[]{:S(2)}) copy-start(bf16[192,1024]{1,0:T(8,128)(2,1)} %value.3) | copy-start | bytes 1179652
  10.6 33.9 %collective-permute-start.3 = (bf16[400,1024]{1,0:T(8,128)(2,1)S(1)}, bf16[400,1024]{1,0:T(8,128)(2,1)S(1)}, u32[]{:S(2)}, u32[]{:S(2)}) collective-permute-start(bf16[400,1024]{1,0:T(8,128)(2,1)S(1)} %get-tuple-element.13), channel_id=1, source_target_pairs={{0,2},{1,3},{2,4},{3,5},{4,6},{5,7},{6,8},{7,9},{8,10},{9,11},{10,... | collective-permute-start | bytes 2457608 | tf_op jit(solution)/shard_map/ppermute | solution.py:22
  12.8 38.7 %collective-permute-start.7 = (bf16[1024,512]{1,0:T(8,128)(2,1)S(1)}, bf16[1024,512]{1,0:T(8,128)(2,1)S(1)}, u32[]{:S(2)}, u32[]{:S(2)}) collective-permute-start(bf16[1024,512]{1,0:T(8,128)(2,1)S(1)} %copy-done.1), channel_id=1, source_target_pairs={{0,1},{1,0},{2,3},{3,2},{4,5},{5,4},{6,7},{7,6},{8,9},{9,8},{10,11... | collective-permute-start | bytes 3145736 | tf_op jit(solution)/shard_map/ppermute | solution.py:27
  16.5 25.3 %collective-permute-start.9 = (bf16[512,512]{1,0:T(8,128)(2,1)S(1)}, bf16[512,512]{1,0:T(8,128)(2,1)S(1)}, u32[]{:S(2)}, u32[]{:S(2)}) collective-permute-start(bf16[512,512]{1,0:T(8,128)(2,1)S(1)} %collective-permute-done.8.refs_2_), channel_id=1, source_target_pairs={{0,4},{1,5},{2,10},{3,11},{4,0},{5,1},{6,14},{7,15},{8,12},{9,13},... | collective-permute-start | bytes 1572872 | tf_op jit(solution)/shard_map/ppermute | solution.py:50
  34.7 16.9 %copy-start.9 = (f32[2048]{0:T(1024)S(1)}, f32[2048]{0:T(1024)}, u32[]{:S(2)}) copy-start(f32[2048]{0:T(1024)} %param.15) | copy-start | bytes 24580
  34.7 9.9 %collective-permute-start.4 = (bf16[144,1024]{1,0:T(8,128)(2,1)S(1)}, bf16[144,1024]{1,0:T(8,128)(2,1)S(1)}, u32[]{:S(2)}, u32[]{:S(2)}) collective-permute-start(bf16[144,1024]{1,0:T(8,128)(2,1)S(1)} %get-tuple-element.14), channel_id=1, source_target_pairs={{0,4},{1,5},{2,6},{3,7},{4,8},{5,9},{6,10},{7,11},{8,12},{9,13},{1... | collective-permute-start | bytes 884744 | tf_op jit(solution)/shard_map/ppermute | solution.py:22
  36.7 14.8 %collective-permute-start.10 = (bf16[512,512]{1,0:T(8,128)(2,1)S(1)}, bf16[512,512]{1,0:T(8,128)(2,1)S(1)}, u32[]{:S(2)}, u32[]{:S(2)}) collective-permute-start(bf16[512,512]{1,0:T(8,128)(2,1)S(1)} %collective-permute-done.8.refs_2_), channel_id=1, source_target_pairs={{0,1},{1,0},{2,3},{3,2},{4,5},{5,4},{6,7},{7,6},{8,9},{9,8},{10,11... | collective-permute-start | bytes 1572872 | tf_op jit(solution)/shard_map/ppermute | solution.py:27
  41.8 9.7 %collective-permute-start.11 = (bf16[512,512]{1,0:T(8,128)(2,1)S(1)}, bf16[512,512]{1,0:T(8,128)(2,1)S(1)}, u32[]{:S(2)}, u32[]{:S(2)}) collective-permute-start(bf16[512,512]{1,0:T(8,128)(2,1)S(1)} %collective-permute-done.9.refs_3_), channel_id=1, source_target_pairs={{0,1},{1,0},{2,3},{3,2},{4,5},{5,4},{6,7},{7,6},{8,9},{9,8},{10,11... | collective-permute-start | bytes 1572872 | tf_op jit(solution)/shard_map/ppermute | solution.py:27
  48.2 3.4 %collective-permute-start.5 = (bf16[208,512]{1,0:T(8,128)(2,1)S(1)}, bf16[208,512]{1,0:T(8,128)(2,1)S(1)}, u32[]{:S(2)}, u32[]{:S(2)}) collective-permute-start(bf16[208,512]{1,0:T(8,128)(2,1)S(1)} %get-tuple-element.16), channel_id=1, source_target_pairs={{0,1},{1,0},{2,3},{3,2},{4,5},{5,4},{6,7},{7,6},{8,9},{9,8},{10,11... | collective-permute-start | bytes 638984 | tf_op jit(solution)/shard_map/ppermute | solution.py:27
  48.2 3.3 %collective-permute-start.6 = (bf16[16,2048]{1,0:T(8,128)(2,1)S(1)}, bf16[16,2048]{1,0:T(8,128)(2,1)S(1)}, u32[]{:S(2)}, u32[]{:S(2)}) collective-permute-start(bf16[16,2048]{1,0:T(8,128)(2,1)S(1)} %get-tuple-element.17), channel_id=1, source_target_pairs={{0,1},{1,2},{2,3},{3,4},{4,5},{5,6},{6,7},{7,8},{8,9},{9,10},{10,1... | collective-permute-start | bytes 196616 | tf_op jit(solution)/shard_map/ppermute | solution.py:22
  51.5 12.2 %copy-start.10 = (bf16[2048,128]{1,0:T(8,128)(2,1)S(1)}, bf16[2048,128]{1,0:T(8,128)(2,1)}, u32[]{:S(2)}) copy-start(bf16[2048,128]{1,0:T(8,128)(2,1)} %param.18) | copy-start | bytes 1572868
  51.6 12.2 %copy-start.11 = (bf16[2048,128]{1,0:T(8,128)(2,1)S(1)}, bf16[2048,128]{1,0:T(8,128)(2,1)}, u32[]{:S(2)}) copy-start(bf16[2048,128]{1,0:T(8,128)(2,1)} %param.17) | copy-start | bytes 1572868
  51.6 12.2 %copy-start.12 = (bf16[2048,128]{1,0:T(8,128)(2,1)S(1)}, bf16[2048,128]{1,0:T(8,128)(2,1)}, u32[]{:S(2)}) copy-start(bf16[2048,128]{1,0:T(8,128)(2,1)} %param.16) | copy-start | bytes 1572868
  63.8 23.1 %copy-start.8 = (bf16[128,2048]{1,0:T(8,128)(2,1)S(1)}, bf16[128,2048]{1,0:T(8,128)(2,1)}, u32[]{:S(2)}) copy-start(bf16[128,2048]{1,0:T(8,128)(2,1)} %w_out.1) | copy-start | bytes 1572868
  64.2 9.1 %collective-permute-start.12 = (bf16[96,256]{1,0:T(8,128)(2,1)S(1)}, bf16[96,256]{1,0:T(8,128)(2,1)S(1)}, u32[]{:S(2)}, u32[]{:S(2)}) collective-permute-start(bf16[96,256]{1,0:T(8,128)(2,1)S(1)} %slice.9), channel_id=1, source_target_pairs={{0,4},{4,0},{8,12},{12,8},{16,20},{20,16},{24,28},{28,24},{1,5},{5... | collective-permute-start | bytes 147464 | tf_op jit(solution)/shard_map/ppermute | solution.py:61
  73.3 7.2 %collective-permute-start.13 = (bf16[192,256]{1,0:T(8,128)(2,1)S(1)}, bf16[192,256]{1,0:T(8,128)(2,1)S(1)}, u32[]{:S(2)}, u32[]{:S(2)}) collective-permute-start(bf16[192,256]{1,0:T(8,128)(2,1)S(1)} %pad_maximum_fusion.refs_0_), channel_id=1, source_target_pairs={{0,8},{4,12},{8,0},{12,4},{16,24},{20,28},{24,16},{28,20},{1,9},{5... | collective-permute-start | bytes 294920 | tf_op jit(solution)/shard_map/ppermute | solution.py:64
  77.1 9.8 %collective-permute-start.14 = (bf16[192,256]{1,0:T(8,128)(2,1)S(1)}, bf16[192,256]{1,0:T(8,128)(2,1)S(1)}, u32[]{:S(2)}, u32[]{:S(2)}) collective-permute-start(bf16[192,256]{1,0:T(8,128)(2,1)S(1)} %pad_maximum_fusion.refs_0_), channel_id=1, source_target_pairs={{0,16},{4,20},{8,24},{12,28},{16,0},{20,4},{24,8},{28,12},{1,17},{... | collective-permute-start | bytes 294920 | tf_op jit(solution)/shard_map/ppermute | solution.py:64
  79.7 7.2 %collective-permute-start.15 = (bf16[192,256]{1,0:T(8,128)(2,1)S(1)}, bf16[192,256]{1,0:T(8,128)(2,1)S(1)}, u32[]{:S(2)}, u32[]{:S(2)}) collective-permute-start(bf16[192,256]{1,0:T(8,128)(2,1)S(1)} %pad_maximum_fusion.refs_0_), channel_id=1, source_target_pairs={{0,24},{4,28},{8,16},{12,20},{16,8},{20,12},{24,0},{28,4},{1,25},{... | collective-permute-start | bytes 294920 | tf_op jit(solution)/shard_map/ppermute | solution.py:64
  88.4 5.2 %collective-permute-start.18 = (bf16[24,2048]{1,0:T(8,128)(2,1)S(1)}, bf16[24,2048]{1,0:T(8,128)(2,1)S(1)}, u32[]{:S(2)}, u32[]{:S(2)}) collective-permute-start(bf16[24,2048]{1,0:T(8,128)(2,1)S(1)} %get-tuple-element.22), channel_id=1, source_target_pairs={{0,3},{1,2},{2,1},{3,0},{4,7},{5,6},{6,5},{7,4},{8,11},{9,10},{10,... | collective-permute-start | bytes 294920 | tf_op jit(solution)/shard_map/ppermute | solution.py:138
  88.4 6.6 %collective-permute-start.17 = (bf16[24,2048]{1,0:T(8,128)(2,1)S(1)}, bf16[24,2048]{1,0:T(8,128)(2,1)S(1)}, u32[]{:S(2)}, u32[]{:S(2)}) collective-permute-start(bf16[24,2048]{1,0:T(8,128)(2,1)S(1)} %get-tuple-element.23), channel_id=1, source_target_pairs={{0,2},{1,3},{2,0},{3,1},{4,6},{5,7},{6,4},{7,5},{8,10},{9,11},{10,... | collective-permute-start | bytes 294920 | tf_op jit(solution)/shard_map/ppermute | solution.py:138
  89.7 5.4 %collective-permute-start.16 = (bf16[24,2048]{1,0:T(8,128)(2,1)S(1)}, bf16[24,2048]{1,0:T(8,128)(2,1)S(1)}, u32[]{:S(2)}, u32[]{:S(2)}) collective-permute-start(bf16[24,2048]{1,0:T(8,128)(2,1)S(1)} %get-tuple-element.21), channel_id=1, source_target_pairs={{0,1},{1,0},{2,3},{3,2},{4,5},{5,4},{6,7},{7,6},{8,9},{9,8},{10,11... | collective-permute-start | bytes 294920 | tf_op jit(solution)/shard_map/ppermute | solution.py:138
